TPU v7x, 32 devices: a whole 2x2x4 slice. The times are simulated.
32 devices in a mesh: ctx: 4 (over y, core), shard: 8 (over z, x).
Axes of the slice: x: 2, y: 2, z: 4, core: 2. Of those that a mesh axis runs over, the one named last changes fastest.
Arguments:
- block_input: bfloat16 [8, 1024, 1024], P('shard', 'ctx'), may hold values from -6 to 6
- lengths: int32 [8], P('shard'), may hold values from 256 to 1024, as said below
- mem_keep: float32 [8, 8], P('shard', 'ctx'), may hold values from 0.9 to 0.999
- mem_momentum: float32 [8, 8], P('shard', 'ctx'), may hold values from 0.5 to 0.8
- mem_rate: float32 [8, 8], P('shard', 'ctx'), may hold values from 0.002 to 0.01
- norm_gain: bfloat16 [1024], P('shard'), may hold values from 0.5 to 1.5
- w_query: bfloat16 [1024, 1024], P('shard'), may hold values from -0.1875 to 0.1875
- w_key: bfloat16 [1024, 1024], P('shard'), may hold values from -0.1875 to 0.1875
- w_value: bfloat16 [1024, 1024], P('shard'), may hold values from -0.1875 to 0.1875
- persist_keys: bfloat16 [16, 1024], P(None, 'shard'), may hold values from -6 to 6
- persist_values: bfloat16 [16, 1024], P(None, 'shard'), may hold values from -6 to 6
- w_out: bfloat16 [1024, 1024], P('shard'), may hold values from -6 to 6
- mem_query: bfloat16 [1024, 1024], P('shard'), may hold values from -0.1875 to 0.1875
- mem_key: bfloat16 [1024, 1024], P('shard'), may hold values from -0.1875 to 0.1875
- mem_value: bfloat16 [1024, 1024], P('shard'), may hold values from -0.1875 to 0.1875
- mem_first: bfloat16 [1024, 1024], P('shard'), may hold values from -0.1875 to 0.1875
- mem_second: bfloat16 [1024, 1024], P('shard'), may hold values from -0.1875 to 0.1875
- ffn_gain: bfloat16 [1024], P('shard'), may hold values from 0.5 to 1.5
- w_gate: bfloat16 [1024, 2816], P('shard'), may hold values from -0.1875 to 0.1875
- w_up: bfloat16 [1024, 2816], P('shard'), may hold values from -0.1875 to 0.1875
- w_down: bfloat16 [2816, 1024], P('shard'), may hold values from -0.109375 to 0.109375
- cotangent: bfloat16 [8, 1024, 1024], P('shard', 'ctx'), may hold values from -6 to 6
Outputs:
- output: bfloat16 [8, 1024, 1024], P('shard', 'ctx')
- input_grad: bfloat16 [8, 1024, 1024], P('shard', 'ctx')
- grad_norm_gain: float32 [1024], P(('ctx', 'shard'))
- grad_w_query: float32 [1024, 1024], P(('ctx', 'shard'))
- grad_w_key: float32 [1024, 1024], P(('ctx', 'shard'))
- grad_w_value: float32 [1024, 1024], P(('ctx', 'shard'))
- grad_persist_keys: float32 [16, 1024], P(None, ('ctx', 'shard'))
- grad_persist_values: float32 [16, 1024], P(None, ('ctx', 'shard'))
- grad_w_out: float32 [1024, 1024], P(('ctx', 'shard'))
- grad_mem_query: float32 [1024, 1024], P(('ctx', 'shard'))
- grad_mem_key: float32 [1024, 1024], P(('ctx', 'shard'))
- grad_mem_value: float32 [1024, 1024], P(('ctx', 'shard'))
- grad_mem_first: float32 [1024, 1024], P(('ctx', 'shard'))
- grad_mem_second: float32 [1024, 1024], P(('ctx', 'shard'))
- grad_ffn_gain: float32 [1024], P(('ctx', 'shard'))
- grad_w_gate: float32 [1024, 2816], P(('ctx', 'shard'))
- grad_w_up: float32 [1024, 2816], P(('ctx', 'shard'))
- grad_w_down: float32 [2816, 1024], P(('ctx', 'shard'))
Inputs may be any that keep to these rules, and one draw needn't show every extreme that they name: `lengths`: each length is a multiple of 128; in every draw some sequence has length 1024.
All inputs are finite; a program needn't handle non-finite values.
Results may differ from a plain program's by a relative error of at most 0.02.
Values may be sent and summed in bfloat16 or wider, within the bound.
No kernel may reach another device: no remote copies, remote signals or barrier semaphores. Data moves between devices by JAX's collectives and lax.ppermute only.
A program may use at most 512 MiB of HBM per device.

v0:
```python
import jax
import jax.numpy as jnp
from jax import lax
from jax.sharding import PartitionSpec as P

HEADS = 8
HEAD_DIM = 128
WINDOW = 1024
SPAN = 128


highest = lax.Precision.HIGHEST


def from_behind(value, axis, steps):
    count = lax.axis_size(axis)
    first, last = (max(0, -steps), min(count, count - steps))
    return lax.ppermute(value, axis, [(source, source + steps) for source in range(first, last)])


def as_sent(x):

    def short(part):
        return part.astype(jnp.bfloat16) if part.dtype == jnp.float32 else part

    return jax.tree.map(short, x)


def matmul(left, right):
    return jnp.dot(left, right, precision=highest)


def rms_norm(values, gain):
    return values * lax.rsqrt(jnp.mean(values * values, axis=-1, keepdims=True) + 1e-05) * gain


def silu_slope(inputs):
    sigma = jax.nn.sigmoid(inputs)
    return sigma * (1.0 + inputs * (1.0 - sigma))


def product_swap(left, right):
    return lax.dot_general(
        left, right, (((0,), (0,)), ((), ())), preferred_element_type=jnp.float32
    )


def product_back(left, right):
    return lax.dot_general(
        left, right, (((1,), (1,)), ((), ())), preferred_element_type=jnp.float32
    )


def product(left, right):
    return jnp.dot(left, right, preferred_element_type=jnp.float32)


def memory_span(state, inputs):
    first, second, speed_first, speed_second = state
    query_rows, key_rows, value_rows, alive, keep, momentum, rate = inputs
    recalled = matmul(jax.nn.silu(matmul(query_rows, first)), second)
    hidden_pre = matmul(key_rows, first)
    hidden_act = jax.nn.silu(hidden_pre)
    error = (matmul(hidden_act, second) - value_rows) * alive[:, None] / SPAN
    grad_second = matmul(hidden_act.T, error)
    grad_first = matmul(key_rows.T, matmul(error, second.T) * silu_slope(hidden_pre))
    speed_first = momentum * speed_first - rate * grad_first
    speed_second = momentum * speed_second - rate * grad_second
    first = keep * first + speed_first
    second = keep * second + speed_second
    return ((first, second, speed_first, speed_second), recalled)


def memory_segment(state, query_rows, key_rows, value_rows, alive, keep, momentum, rate):
    count = alive.shape[0] // SPAN
    shaped = (
        query_rows.reshape(count, SPAN, -1),
        key_rows.reshape(count, SPAN, -1),
        value_rows.reshape(count, SPAN, -1),
        alive.reshape(count, SPAN),
        keep,
        momentum,
        rate,
    )
    state, recalled = lax.scan(jax.checkpoint(memory_span), state, shaped)
    return (state, recalled.reshape(alive.shape[0], -1))


def attend_scores(query_heads, key_heads, allowed):
    scores = jnp.einsum(
        "thd,shd->hts", query_heads, key_heads, preferred_element_type=jnp.float32
    ) * HEAD_DIM ** (-0.5)
    return jnp.where(allowed[None], scores, -1e30)


def on_device(
    block_input,
    lengths,
    mem_keep,
    mem_momentum,
    mem_rate,
    norm_gain,
    w_query,
    w_key,
    w_value,
    persist_keys,
    persist_values,
    w_out,
    mem_query,
    mem_key,
    mem_value,
    mem_first,
    mem_second,
    ffn_gain,
    w_gate,
    w_up,
    w_down,
    cotangent,
):
    bundle = (
        lax.all_gather(norm_gain, "shard", axis=0, tiled=True),
        lax.all_gather(w_query, "shard", axis=0, tiled=True),
        lax.all_gather(w_key, "shard", axis=0, tiled=True),
        lax.all_gather(w_value, "shard", axis=0, tiled=True),
        lax.all_gather(persist_keys, "shard", axis=1, tiled=True),
        lax.all_gather(persist_values, "shard", axis=1, tiled=True),
        lax.all_gather(w_out, "shard", axis=0, tiled=True),
        lax.all_gather(mem_query, "shard", axis=0, tiled=True),
        lax.all_gather(mem_key, "shard", axis=0, tiled=True),
        lax.all_gather(mem_value, "shard", axis=0, tiled=True),
        lax.all_gather(mem_first, "shard", axis=0, tiled=True),
        lax.all_gather(mem_second, "shard", axis=0, tiled=True),
        lax.all_gather(ffn_gain, "shard", axis=0, tiled=True),
        lax.all_gather(w_gate, "shard", axis=0, tiled=True),
        lax.all_gather(w_up, "shard", axis=0, tiled=True),
        lax.all_gather(w_down, "shard", axis=0, tiled=True),
    )
    (
        all_gain,
        all_query,
        all_key,
        all_value,
        all_pkeys,
        all_pvalues,
        all_out,
        all_mquery,
        all_mkey,
        all_mvalue,
        all_first,
        all_second,
        all_gain_two,
        all_gate,
        all_upper,
        all_down,
    ) = bundle
    tokens = block_input[0].astype(jnp.float32)
    rows = tokens.shape[0]
    width = tokens.shape[1]
    ctx_index = lax.axis_index("ctx")
    ctx_count = lax.axis_size("ctx")
    length = lengths[0]
    positions = ctx_index * rows + jnp.arange(rows, dtype=jnp.int32)
    alive = (positions < length).astype(jnp.float32)
    gain_one = all_gain.astype(jnp.float32)
    normed = rms_norm(tokens, gain_one).astype(jnp.bfloat16)
    queries = product(normed, all_query).astype(jnp.bfloat16)
    keys_local = product(normed, all_key).astype(jnp.bfloat16)
    values_local = product(normed, all_value).astype(jnp.bfloat16)
    mquery = product(normed, all_mquery).astype(jnp.bfloat16)
    mkey = product(normed, all_mkey).astype(jnp.bfloat16)
    mvalue = product(normed, all_mvalue).astype(jnp.bfloat16)
    reach = min(WINDOW // rows, ctx_count - 1)
    local_pair = jnp.stack([keys_local, values_local])
    remote = []
    current = local_pair
    for offset in range(reach):
        current = from_behind(current, "ctx", 1)
        remote.append(current)
    blocks = [remote[offset - 1] for offset in range(reach, 0, -1)] + [local_pair]
    joined = jnp.concatenate(blocks, axis=1)
    persist_count = all_pkeys.shape[0]
    key_heads = jnp.concatenate([all_pkeys, joined[0]], 0).reshape(-1, HEADS, HEAD_DIM)
    value_heads = jnp.concatenate([all_pvalues, joined[1]], 0).reshape(-1, HEADS, HEAD_DIM)
    key_slots = jnp.concatenate(
        [
            (ctx_index - offset) * rows + jnp.arange(rows, dtype=jnp.int32)
            for offset in range(reach, -1, -1)
        ]
    )
    window_ok = (key_slots[None, :] <= positions[:, None]) & (
        positions[:, None] - key_slots[None, :] < WINDOW
    )
    window_ok = window_ok & (key_slots[None, :] >= 0) & (key_slots[None, :] < length)
    allowed = jnp.concatenate([jnp.ones((rows, persist_count), dtype=bool), window_ok], 1)
    query_heads = queries.reshape(rows, HEADS, HEAD_DIM)
    scores = attend_scores(query_heads, key_heads, allowed)
    peak = jnp.max(scores, axis=-1, keepdims=True)
    exponent = jnp.exp(scores - peak)
    total = jnp.sum(exponent, axis=-1, keepdims=True)
    log_total = peak + jnp.log(total)
    probs = (exponent / total).astype(jnp.bfloat16)
    attended = jnp.einsum(
        "hts,shd->thd", probs, value_heads, preferred_element_type=jnp.float32
    ).reshape(rows, width)
    mquery_f = mquery.astype(jnp.float32)
    mkey_f = mkey.astype(jnp.float32)
    mvalue_f = mvalue.astype(jnp.float32)
    keep_rows = mem_keep[0]
    momentum_rows = mem_momentum[0]
    rate_rows = mem_rate[0]
    first_init = all_first.astype(jnp.float32)
    second_init = all_second.astype(jnp.float32)
    state_start = (first_init, second_init, jnp.zeros_like(first_init), jnp.zeros_like(second_init))
    zero_rows = jnp.zeros((rows, width), jnp.float32)

    def run_segment(state):
        return memory_segment(
            state, mquery_f, mkey_f, mvalue_f, alive, keep_rows, momentum_rows, rate_rows
        )

    def pass_segment(state):
        return (state, zero_rows)

    state_in = state_start
    recalled = zero_rows
    for step in range(ctx_count):
        state_out, recalled_part = lax.cond(ctx_index == step, run_segment, pass_segment, state_in)
        recalled = recalled + recalled_part
        if step + 1 < ctx_count:
            received = jax.tree.map(
                lambda part, own: part.astype(own.dtype),
                from_behind(as_sent(state_out), "ctx", 1),
                state_out,
            )
            state_in = jax.tree.map(
                lambda fresh, older: jnp.where(ctx_index == step + 1, fresh, older),
                received,
                state_in,
            )
    combined = (attended * recalled).astype(jnp.bfloat16)
    middle = tokens + product(combined, all_out)
    gain_two = all_gain_two.astype(jnp.float32)
    normed_two = rms_norm(middle, gain_two).astype(jnp.bfloat16)
    gate = product(normed_two, all_gate)
    upper = product(normed_two, all_upper)
    activated = (jax.nn.silu(gate) * upper).astype(jnp.bfloat16)
    result = alive[:, None] * (middle + product(activated, all_down))
    later = (
        lax.all_gather(norm_gain, "shard", axis=0, tiled=True),
        lax.all_gather(w_query, "shard", axis=0, tiled=True),
        lax.all_gather(w_key, "shard", axis=0, tiled=True),
        lax.all_gather(w_value, "shard", axis=0, tiled=True),
        lax.all_gather(persist_keys, "shard", axis=1, tiled=True),
        lax.all_gather(persist_values, "shard", axis=1, tiled=True),
        lax.all_gather(w_out, "shard", axis=0, tiled=True),
        lax.all_gather(mem_query, "shard", axis=0, tiled=True),
        lax.all_gather(mem_key, "shard", axis=0, tiled=True),
        lax.all_gather(mem_value, "shard", axis=0, tiled=True),
        lax.all_gather(mem_first, "shard", axis=0, tiled=True),
        lax.all_gather(mem_second, "shard", axis=0, tiled=True),
        lax.all_gather(ffn_gain, "shard", axis=0, tiled=True),
        lax.all_gather(w_gate, "shard", axis=0, tiled=True),
        lax.all_gather(w_up, "shard", axis=0, tiled=True),
        lax.all_gather(w_down, "shard", axis=0, tiled=True),
    )
    (
        back_gain,
        back_query,
        back_key,
        back_value,
        back_pkeys,
        back_pvalues,
        back_out,
        back_mquery,
        back_mkey,
        back_mvalue,
        back_first,
        back_second,
        back_gain_two,
        back_gate,
        back_upper,
        back_down,
    ) = later
    d_result = cotangent[0].astype(jnp.float32) * alive[:, None]
    d_ffn = d_result.astype(jnp.bfloat16)
    grad_down = product_swap(activated, d_ffn)
    d_act = product_back(d_ffn, back_down)
    _, pull_act = jax.vjp(lambda gate_in, upper_in: jax.nn.silu(gate_in) * upper_in, gate, upper)
    d_gate, d_upper = pull_act(d_act)
    d_gate = d_gate.astype(jnp.bfloat16)
    d_upper = d_upper.astype(jnp.bfloat16)
    grad_gate = product_swap(normed_two, d_gate)
    grad_upper = product_swap(normed_two, d_upper)
    d_normed_two = product_back(d_gate, back_gate) + product_back(d_upper, back_upper)
    _, pull_two = jax.vjp(rms_norm, middle, back_gain_two.astype(jnp.float32))
    d_middle_norm, grad_gain_two = pull_two(d_normed_two)
    ffn_sums = (
        lax.psum_scatter(grad_gain_two, ("ctx", "shard"), scatter_dimension=0, tiled=True),
        lax.psum_scatter(grad_gate, ("ctx", "shard"), scatter_dimension=0, tiled=True),
        lax.psum_scatter(grad_upper, ("ctx", "shard"), scatter_dimension=0, tiled=True),
        lax.psum_scatter(grad_down, ("ctx", "shard"), scatter_dimension=0, tiled=True),
    )
    d_middle = d_result + d_middle_norm
    d_branch = d_middle.astype(jnp.bfloat16)
    grad_out = product_swap(combined, d_branch)
    d_combined = product_back(d_branch, back_out)
    d_attended = (d_combined * recalled).astype(jnp.bfloat16)
    d_recalled = d_combined * attended
    d_heads = d_attended.reshape(rows, HEADS, HEAD_DIM)
    scores = attend_scores(query_heads, key_heads, allowed)
    probs_full = jnp.exp(scores - log_total)
    probs_low = probs_full.astype(jnp.bfloat16)
    d_probs = jnp.einsum("thd,shd->hts", d_heads, value_heads, preferred_element_type=jnp.float32)
    centre = jnp.sum(d_probs * probs_full, axis=-1, keepdims=True)
    d_scores = (probs_full * (d_probs - centre)).astype(jnp.bfloat16)
    scale = HEAD_DIM ** (-0.5)
    d_queries = (
        scale * jnp.einsum("hts,shd->thd", d_scores, key_heads, preferred_element_type=jnp.float32)
    ).reshape(rows, width)
    d_keys_all = (
        scale
        * jnp.einsum("hts,thd->shd", d_scores, query_heads, preferred_element_type=jnp.float32)
    ).reshape(-1, width)
    d_values_all = jnp.einsum(
        "hts,thd->shd", probs_low, d_heads, preferred_element_type=jnp.float32
    ).reshape(-1, width)
    grad_pkeys = d_keys_all[:persist_count]
    grad_pvalues = d_values_all[:persist_count]

    def block_grads(offset):
        begin = persist_count + (reach - offset) * rows
        return jnp.stack([d_keys_all[begin : begin + rows], d_values_all[begin : begin + rows]])

    gathered_grads = block_grads(reach)
    for offset in range(reach - 1, -1, -1):
        gathered_grads = from_behind(gathered_grads.astype(jnp.bfloat16), "ctx", -1).astype(
            gathered_grads.dtype
        ) + block_grads(offset)
    d_queries_low = d_queries.astype(jnp.bfloat16)
    d_keys_low = gathered_grads[0].astype(jnp.bfloat16)
    d_values_low = gathered_grads[1].astype(jnp.bfloat16)

    def run_back(operand):
        state, d_state = operand
        _, pull_memory = jax.vjp(
            lambda state_arg, query_arg, key_arg, value_arg: memory_segment(
                state_arg, query_arg, key_arg, value_arg, alive, keep_rows, momentum_rows, rate_rows
            ),
            state,
            mquery_f,
            mkey_f,
            mvalue_f,
        )
        return pull_memory((d_state, d_recalled))

    def skip_back(operand):
        state, d_state = operand
        return (
            jax.tree.map(jnp.zeros_like, state),
            jnp.zeros_like(mquery_f),
            jnp.zeros_like(mkey_f),
            jnp.zeros_like(mvalue_f),
        )

    d_state = jax.tree.map(jnp.zeros_like, state_in)
    d_mquery = jnp.zeros_like(mquery_f)
    d_mkey = jnp.zeros_like(mkey_f)
    d_mvalue = jnp.zeros_like(mvalue_f)
    d_start = d_state
    for step in range(ctx_count - 1, -1, -1):
        d_start, part_query, part_key, part_value = lax.cond(
            ctx_index == step, run_back, skip_back, (state_in, d_state)
        )
        d_mquery = d_mquery + part_query
        d_mkey = d_mkey + part_key
        d_mvalue = d_mvalue + part_value
        if step > 0:
            received = jax.tree.map(
                lambda part, own: part.astype(own.dtype),
                from_behind(as_sent(d_start), "ctx", -1),
                d_start,
            )
            d_state = jax.tree.map(
                lambda fresh, older: jnp.where(ctx_index == step - 1, fresh, older),
                received,
                d_state,
            )
    d_mquery_low = d_mquery.astype(jnp.bfloat16)
    d_mkey_low = d_mkey.astype(jnp.bfloat16)
    d_mvalue_low = d_mvalue.astype(jnp.bfloat16)
    grad_query = product_swap(normed, d_queries_low)
    grad_key = product_swap(normed, d_keys_low)
    grad_value = product_swap(normed, d_values_low)
    grad_mquery = product_swap(normed, d_mquery_low)
    grad_mkey = product_swap(normed, d_mkey_low)
    grad_mvalue = product_swap(normed, d_mvalue_low)
    d_normed = (
        product_back(d_queries_low, back_query)
        + product_back(d_keys_low, back_key)
        + product_back(d_values_low, back_value)
    )
    d_normed = (
        d_normed
        + product_back(d_mquery_low, back_mquery)
        + product_back(d_mkey_low, back_mkey)
        + product_back(d_mvalue_low, back_mvalue)
    )
    _, pull_one = jax.vjp(rms_norm, tokens, back_gain.astype(jnp.float32))
    d_tokens_norm, grad_gain_one = pull_one(d_normed)
    d_tokens = d_middle + d_tokens_norm
    main_sums = (
        lax.psum_scatter(grad_gain_one, ("ctx", "shard"), scatter_dimension=0, tiled=True),
        lax.psum_scatter(grad_query, ("ctx", "shard"), scatter_dimension=0, tiled=True),
        lax.psum_scatter(grad_key, ("ctx", "shard"), scatter_dimension=0, tiled=True),
        lax.psum_scatter(grad_value, ("ctx", "shard"), scatter_dimension=0, tiled=True),
        lax.psum_scatter(grad_pkeys, ("ctx", "shard"), scatter_dimension=1, tiled=True),
        lax.psum_scatter(grad_pvalues, ("ctx", "shard"), scatter_dimension=1, tiled=True),
        lax.psum_scatter(grad_out, ("ctx", "shard"), scatter_dimension=0, tiled=True),
        lax.psum_scatter(grad_mquery, ("ctx", "shard"), scatter_dimension=0, tiled=True),
        lax.psum_scatter(grad_mkey, ("ctx", "shard"), scatter_dimension=0, tiled=True),
        lax.psum_scatter(grad_mvalue, ("ctx", "shard"), scatter_dimension=0, tiled=True),
        lax.psum_scatter(d_start[0], ("ctx", "shard"), scatter_dimension=0, tiled=True),
        lax.psum_scatter(d_start[1], ("ctx", "shard"), scatter_dimension=0, tiled=True),
    )
    return (
        result.astype(jnp.bfloat16)[None],
        d_tokens.astype(jnp.bfloat16)[None],
        main_sums[0],
        main_sums[1],
        main_sums[2],
        main_sums[3],
        main_sums[4],
        main_sums[5],
        main_sums[6],
        main_sums[7],
        main_sums[8],
        main_sums[9],
        main_sums[10],
        main_sums[11],
        ffn_sums[0],
        ffn_sums[1],
        ffn_sums[2],
        ffn_sums[3],
    )


def solution(mesh):
    in_specs = (
        P("shard", "ctx", None),
        P("shard"),
        P("shard", "ctx"),
        P("shard", "ctx"),
        P("shard", "ctx"),
        P("shard"),
        P("shard", None),
        P("shard", None),
        P("shard", None),
        P(None, "shard"),
        P(None, "shard"),
        P("shard", None),
        P("shard", None),
        P("shard", None),
        P("shard", None),
        P("shard", None),
        P("shard", None),
        P("shard"),
        P("shard", None),
        P("shard", None),
        P("shard", None),
        P("shard", "ctx", None),
    )
    out_specs = (
        P("shard", "ctx", None),
        P("shard", "ctx", None),
        P(("ctx", "shard")),
        P(("ctx", "shard"), None),
        P(("ctx", "shard"), None),
        P(("ctx", "shard"), None),
        P(None, ("ctx", "shard")),
        P(None, ("ctx", "shard")),
        P(("ctx", "shard"), None),
        P(("ctx", "shard"), None),
        P(("ctx", "shard"), None),
        P(("ctx", "shard"), None),
        P(("ctx", "shard"), None),
        P(("ctx", "shard"), None),
        P(("ctx", "shard")),
        P(("ctx", "shard"), None),
        P(("ctx", "shard"), None),
        P(("ctx", "shard"), None),
    )
    return jax.shard_map(
        on_device, mesh=mesh, in_specs=in_specs, out_specs=out_specs, check_vma=False
    )
```

profile of v0, /device:TPU:0, one launch (start us, length us, event | category | flops | bytes accessed | tf_op | source)
XLA Modules:
  0.0 4007.2 jit_solution(3611193895212259510)
XLA Ops:
  15.4 22.3 all-gather
  38.0 24.2 all-gather.17.cloned.1.call-done
  64.6 47.6 %all-gather.15.cloned.1.call-done = bf16[1024,1024]{1,0:T(8,128)(2,1)} async-done(((bf16[128,1024]{1,0:T(8,128)(2,1)}), bf16[1024,1024]{1,0:T(8,128)(2,1)}) %all-gather.15.cloned.1.call-update) | async-done | bytes 2097168 | tf_op jit(solution)/shard_map/all_gather | solution.py:123
  117.9 44.1 %all-gather.23.cloned.1.call-done = bf16[1024,1024]{1,0:T(8,128)(2,1)} async-done(((bf16[128,1024]{1,0:T(8,128)(2,1)}), bf16[1024,1024]{1,0:T(8,128)(2,1)}) %all-gather.23.cloned.1.call-update) | async-done | bytes 2097168 | tf_op jit(solution)/shard_map/all_gather | solution.py:132
  166.2 45.7 %all-gather.21.cloned.1.call-done = bf16[1024,1024]{1,0:T(8,128)(2,1)} async-done(((bf16[128,1024]{1,0:T(8,128)(2,1)}), bf16[1024,1024]{1,0:T(8,128)(2,1)}) %all-gather.21.cloned.1.call-update) | async-done | bytes 2097168 | tf_op jit(solution)/shard_map/all_gather | solution.py:131
  215.9 45.7 %all-gather.25.cloned.1.call-done = bf16[1024,1024]{1,0:T(8,128)(2,1)} async-done(((bf16[128,1024]{1,0:T(8,128)(2,1)}), bf16[1024,1024]{1,0:T(8,128)(2,1)}) %all-gather.25.cloned.1.call-update) | async-done | bytes 2097168 | tf_op jit(solution)/shard_map/all_gather | solution.py:128
  264.0 47.4 %all-gather.27.cloned.1.call-done = bf16[1024,1024]{1,0:T(8,128)(2,1)} async-done(((bf16[128,1024]{1,0:T(8,128)(2,1)}), bf16[1024,1024]{1,0:T(8,128)(2,1)}) %all-gather.27.cloned.1.call-update) | async-done | bytes 2097168 | tf_op jit(solution)/shard_map/all_gather | solution.py:129
  313.8 47.6 %all-gather.29.cloned.1.call-done = bf16[1024,1024]{1,0:T(8,128)(2,1)} async-done(((bf16[128,1024]{1,0:T(8,128)(2,1)}), bf16[1024,1024]{1,0:T(8,128)(2,1)}) %all-gather.29.cloned.1.call-update) | async-done | bytes 2097168 | tf_op jit(solution)/shard_map/all_gather | solution.py:130
  363.9 77.5 %conditional.8 = (f32[1024,1024]{1,0:T(8,128)}, f32[1024,1024]{1,0:T(8,128)}, f32[1024,1024]{1,0:T(8,128)}, f32[1024,1024]{1,0:T(8,128)}, f32[256,1024]{1,0:T(8,128)}) conditional(s32[]{:T(128)} %convert_element_type.333, (f32[1024,1024]{1,0:T(8,128)}, f32[1024,1024]{1,0:T(8,128)}) %tuple.203, (f32[256,1024]{1,0:T(8,128)S(1)}, ...), branch_computations={%region_3.4_spmd, %region_4.7_spmd} | conditional | flops 11289886720 | bytes 130025464 | solution.py:227
  364.0 77.0 %while.263 = (s32[]{:T(128)}, f32[1024,1024]{1,0:T(8,128)}, f32[1024,1024]{1,0:T(8,128)}, f32[1024,1024]{1,0:T(8,128)}, f32[1024,1024]{1,0:T(8,128)}, /*index=5*...) while((s32[]{:T(128)}, f32[1024,1024]{1,0:T(8,128)}, ...), condition=%wide.region_6.6_spmd.clone, body=%wide.region_5.5_spmd.clone.sunk | while | flops 11289886720 | bytes 130025296 | solution.py:85
  420.0 9.5 multiply_add_fusion.49
  429.5 9.5 multiply_add_fusion.48
  461.6 18.2 all-gather.1
  485.5 26.5 all_gather.65
  512.0 26.5 all_gather.60
  557.3 20.1 conditional.9
  581.3 25.0 collective-permute-start.10
  653.0 26.9 conditional.10
  683.7 51.2 %collective-permute-start.14 = (bf16[1024,1024]{1,0:T(8,128)(2,1)}, bf16[1024,1024]{1,0:T(8,128)(2,1)}, u32[]{:S(2)}, u32[]{:S(2)}) collective-permute-start(bf16[1024,1024]{1,0:T(8,128)(2,1)} %convert_element_type.367), channel_id=1, source_target_pairs={{0,8},{8,16},{16,24},{1,9},{9,17},{17,25},{2,10},{10,18},{18,26},{... | collective-permute-start | bytes 6291464 | tf_op jit(solution)/shard_map/ppermute | solution.py:18
  743.5 92.1 %collective-permute-start.13 = (bf16[1024,1024]{1,0:T(8,128)(2,1)}, bf16[1024,1024]{1,0:T(8,128)(2,1)}, u32[]{:S(2)}, u32[]{:S(2)}) collective-permute-start(bf16[1024,1024]{1,0:T(8,128)(2,1)} %convert_element_type.365), channel_id=1, source_target_pairs={{0,8},{8,16},{16,24},{1,9},{9,17},{17,25},{2,10},{10,18},{18,26},{... | collective-permute-start | bytes 6291464 | tf_op jit(solution)/shard_map/ppermute | solution.py:18
  879.1 9.6 conditional.11
  936.4 9.4 multiply_convert_fusion
  986.5 32.2 collective-permute-done.15
  1028.1 11.1 collective-permute-done.16
  1048.7 31.6 collective-permute-done.17
  1086.3 18.5 conditional.12
  1148.5 19.7 conditional.13
  1177.7 72.8 %collective-permute-done.25 = bf16[1024,1024]{1,0:T(8,128)(2,1)S(1)} collective-permute-done((bf16[1024,1024]{1,0:T(8,128)(2,1)S(1)}, bf16[1024,1024]{1,0:T(8,128)(2,1)S(1)}, u32[]{:S(2)}, u32[]{:S(2)}) %collective-permute-start.25) | collective-permute-done | bytes 2097184 | tf_op jit(solution)/shard_map/ppermute | solution.py:18
  1267.1 20.2 conditional.14
  1302.7 887.6 %collective-permute-done.29 = bf16[1024,1024]{1,0:T(8,128)(2,1)S(1)} collective-permute-done((bf16[1024,1024]{1,0:T(8,128)(2,1)S(1)}, bf16[1024,1024]{1,0:T(8,128)(2,1)S(1)}, u32[]{:S(2)}, u32[]{:S(2)}) %collective-permute-start.29) | collective-permute-done | bytes 2097184 | tf_op jit(solution)/shard_map/ppermute | solution.py:18
  2203.7 330.0 %conditional.15 = (f32[1024,1024]{1,0:T(8,128)}, f32[1024,1024]{1,0:T(8,128)}, f32[256,1024]{1,0:T(8,128)}, f32[256,1024]{1,0:T(8,128)}, f32[256,1024]{1,0:T(8,128)}) conditional(s32[]{:T(128)} %convert_element_type.333, () %tuple.217, (pred[]{:T(512)}, f32[1024,1024]{1,0:T(8,128)}, f32[1024,1024]{1,0:T(8,128)}, f32[1024,1024]{1,0:T(8,128)}, ...), branch_computations={%region_40.41_spmd, %region_41.46_spmd} | conditional | flops 37096783872 | bytes 496507488 | solution.py:371
  2203.7 9.7 broadcast_select_fusion.2
  2213.4 9.8 broadcast_select_fusion
  2223.1 87.3 %while.261 = (s32[]{:T(128)}, f32[1024,1024]{1,0:T(8,128)}, f32[1024,1024]{1,0:T(8,128)}, f32[1024,1024]{1,0:T(8,128)}, f32[1024,1024]{1,0:T(8,128)}, /*index=5*...) while((s32[]{:T(128)}, f32[1024,1024]{1,0:T(8,128)}, ...), condition=%wide.region_43.43_spmd, body=%wide.region_42.42_spmd.sunk | while | flops 8066039808 | bytes 186648448 | solution.py:85
  2236.7 9.1 multiply_add_fusion.35
  2280.2 9.1 multiply_add_fusion.35
  2313.8 214.6 %while.262 = (s32[]{:T(128)}, f32[1024,1024]{1,0:T(8,128)}, f32[1024,1024]{1,0:T(8,128)}, f32[1024,1024]{1,0:T(8,128)}, f32[1024,1024]{1,0:T(8,128)}, /*index=5*...) while((s32[]{:T(128)}, f32[1024,1024]{1,0:T(8,128)}, ...), condition=%wide.region_45.45_spmd, body=%wide.region_44.44_spmd.sunk | while | flops 29026549760 | bytes 252186992 | solution.py:85
  2411.8 8.9 add_add_fusion.21
  2518.7 8.9 add_add_fusion.21
  2594.1 39.3 all-reduce.3
  2635.6 38.1 reduce-scatter.33.cloned.1.call-done
  2673.7 142.6 %reduce-scatter.35.cloned.1.call-done = f32[32,1024]{1,0:T(8,128)} async-done(((f32[1024,1024]{1,0:T(8,128)}), f32[32,1024]{1,0:T(8,128)}) %reduce-scatter.35.cloned.1.call-update) | async-done | bytes 131088 | tf_op jit(solution)/shard_map/reduce_scatter | solution.py:423
  2816.3 144.2 %reduce-scatter.31.cloned.1.call-done = f32[32,1024]{1,0:T(8,128)} async-done(((f32[1024,1024]{1,0:T(8,128)}), f32[32,1024]{1,0:T(8,128)}) %reduce-scatter.31.cloned.1.call-update) | async-done | bytes 131088 | tf_op jit(solution)/shard_map/reduce_scatter | solution.py:421
  2960.5 143.8 %reduce-scatter.29.cloned.1.call-done = f32[32,1024]{1,0:T(8,128)} async-done(((f32[1024,1024]{1,0:T(8,128)}), f32[32,1024]{1,0:T(8,128)}) %reduce-scatter.29.cloned.1.call-update) | async-done | bytes 131088 | tf_op jit(solution)/shard_map/reduce_scatter | solution.py:420
  3104.3 143.6 %reduce-scatter.27.cloned.1.call-done = f32[32,1024]{1,0:T(8,128)} async-done(((f32[1024,1024]{1,0:T(8,128)}), f32[32,1024]{1,0:T(8,128)}) %reduce-scatter.27.cloned.1.call-update) | async-done | bytes 131088 | tf_op jit(solution)/shard_map/reduce_scatter | solution.py:419
  3247.9 249.5 %reduce-scatter.41.cloned.1.call-done = f32[88,1024]{1,0:T(8,128)} async-done(((f32[2816,1024]{1,0:T(8,128)}), f32[88,1024]{1,0:T(8,128)}) %reduce-scatter.41.cloned.1.call-update) | async-done | bytes 360464 | tf_op jit(solution)/shard_map/reduce_scatter | solution.py:301
  3497.4 252.7 %reduce-scatter.39.cloned.1.call-done = f32[32,2816]{1,0:T(8,128)} async-done(((f32[1024,2816]{1,0:T(8,128)}), f32[32,2816]{1,0:T(8,128)}) %reduce-scatter.39.cloned.1.call-update) | async-done | bytes 360464 | tf_op jit(solution)/shard_map/reduce_scatter | solution.py:300
  3750.1 250.3 %reduce-scatter.37.cloned.1.call-done = f32[32,2816]{1,0:T(8,128)} async-done(((f32[1024,2816]{1,0:T(8,128)}), f32[32,2816]{1,0:T(8,128)}) %reduce-scatter.37.cloned.1.call-update) | async-done | bytes 360464 | tf_op jit(solution)/shard_map/reduce_scatter | solution.py:299
  (629 shorter events, 853.1 us)
Async XLA Ops:
  7.2 55.0 %all-gather.17.cloned.1.call-start = ((), (), s32[]{:S(2)}) async-start(), calls=%async_computation.15 | async-start | bytes 2359296 | tf_op jit(solution)/shard_map/all_gather | solution.py:124
  7.9 104.2 %all-gather.15.cloned.1.call-start = ((), (), s32[]{:S(2)}) async-start(), calls=%async_computation.14 | async-start | bytes 2359296 | tf_op jit(solution)/shard_map/all_gather | solution.py:123
  8.7 153.4 %all-gather.23.cloned.1.call-start = ((), (), s32[]{:S(2)}) async-start(), calls=%async_computation.18 | async-start | bytes 2359296 | tf_op jit(solution)/shard_map/all_gather | solution.py:132
  9.4 202.4 %all-gather.21.cloned.1.call-start = ((), (), s32[]{:S(2)}) async-start(), calls=%async_computation.17 | async-start | bytes 2359296 | tf_op jit(solution)/shard_map/all_gather | solution.py:131
  10.0 251.6 %all-gather.25.cloned.1.call-start = ((), (), s32[]{:S(2)}) async-start(), calls=%async_computation.19 | async-start | bytes 2359296 | tf_op jit(solution)/shard_map/all_gather | solution.py:128
  10.6 300.9 %all-gather.27.cloned.1.call-start = ((), (), s32[]{:S(2)}) async-start(), calls=%async_computation.20 | async-start | bytes 2359296 | tf_op jit(solution)/shard_map/all_gather | solution.py:129
  11.2 350.2 %all-gather.29.cloned.1.call-start = ((), (), s32[]{:S(2)}) async-start(), calls=%async_computation.21 | async-start | bytes 2359296 | tf_op jit(solution)/shard_map/all_gather | solution.py:130
  11.9 595.0 %all-gather.19.cloned.1.call-start = ((), (), s32[]{:S(2)}) async-start(), calls=%async_computation.16 | async-start | bytes 2359296 | tf_op jit(solution)/shard_map/all_gather | solution.py:122
  12.7 880.2 %all-gather.31.cloned.1.call-start = ((), (), s32[]{:S(2)}) async-start(), calls=%async_computation.22 | async-start | bytes 2359296 | tf_op jit(solution)/shard_map/all_gather | solution.py:127
  13.4 883.2 %all-gather.35.cloned.1.call-start = ((), (), s32[]{:S(2)}) async-start(), calls=%async_computation.24 | async-start | bytes 6488064 | tf_op jit(solution)/shard_map/all_gather | solution.py:135
  14.0 888.8 %all-gather.33.cloned.1.call-start = ((), (), s32[]{:S(2)}) async-start(), calls=%async_computation.23 | async-start | bytes 6488064 | tf_op jit(solution)/shard_map/all_gather | solution.py:134
  14.7 894.0 %all-gather.37.cloned.1.call-start = ((), (), s32[]{:S(2)}) async-start(), calls=%async_computation.25 | async-start | bytes 6488064 | tf_op jit(solution)/shard_map/all_gather | solution.py:136
  115.7 343.5 %collective-permute-start = (bf16[2,256,1024]{2,1,0:T(8,128)(2,1)}, bf16[2,256,1024]{2,1,0:T(8,128)(2,1)}, u32[]{:S(2)}, u32[]{:S(2)}) collective-permute-start(bf16[2,256,1024]{2,1,0:T(8,128)(2,1)} %pad_maximum_fusion), channel_id=1, source_target_pairs={{0,8},{8,16},{16,24},{1,9},{9,17},{17,25},{2,10},{10,18},{18,26},{... | collective-permute-start | bytes 3145736 | tf_op jit(solution)/shard_map/ppermute | solution.py:18
  445.5 95.9 %collective-permute-start.5 = (bf16[1024,1024]{1,0:T(8,128)(2,1)}, bf16[1024,1024]{1,0:T(8,128)(2,1)}, u32[]{:S(2)}, u32[]{:S(2)}) collective-permute-start(bf16[1024,1024]{1,0:T(8,128)(2,1)} %convert_element_type.347), channel_id=1, source_target_pairs={{0,8},{8,16},{16,24},{1,9},{9,17},{17,25},{2,10},{10,18},{18,26},{... | collective-permute-start | bytes 6291464 | tf_op jit(solution)/shard_map/ppermute | solution.py:18
  449.7 95.9 %collective-permute-start.4 = (bf16[1024,1024]{1,0:T(8,128)(2,1)}, bf16[1024,1024]{1,0:T(8,128)(2,1)}, u32[]{:S(2)}, u32[]{:S(2)}) collective-permute-start(bf16[1024,1024]{1,0:T(8,128)(2,1)} %convert_element_type.345), channel_id=1, source_target_pairs={{0,8},{8,16},{16,24},{1,9},{9,17},{17,25},{2,10},{10,18},{18,26},{... | collective-permute-start | bytes 6291464 | tf_op jit(solution)/shard_map/ppermute | solution.py:18
  456.5 93.6 %collective-permute-start.6 = (bf16[1024,1024]{1,0:T(8,128)(2,1)}, bf16[1024,1024]{1,0:T(8,128)(2,1)}, u32[]{:S(2)}, u32[]{:S(2)}) collective-permute-start(bf16[1024,1024]{1,0:T(8,128)(2,1)} %convert_element_type.349), channel_id=1, source_target_pairs={{0,8},{8,16},{16,24},{1,9},{9,17},{17,25},{2,10},{10,18},{18,26},{... | collective-permute-start | bytes 6291464 | tf_op jit(solution)/shard_map/ppermute | solution.py:18
  459.2 79.9 %collective-permute-start.1 = (bf16[2,256,1024]{2,1,0:T(8,128)(2,1)}, bf16[2,256,1024]{2,1,0:T(8,128)(2,1)}, u32[]{:S(2)}, u32[]{:S(2)}) collective-permute-start(bf16[2,256,1024]{2,1,0:T(8,128)(2,1)} %collective-permute-done), channel_id=1, source_target_pairs={{0,8},{8,16},{16,24},{1,9},{9,17},{17,25},{2,10},{10,18},{18,26},{... | collective-permute-start | bytes 3145736 | tf_op jit(solution)/shard_map/ppermute | solution.py:18
  461.5 2123.2 %reduce-scatter.45.cloned.1.call-start = ((), (), s32[]{:S(2)}) async-start(), calls=%async_computation.39 | async-start | bytes 540672
  482.9 71.5 %collective-permute-start.3 = (bf16[1024,1024]{1,0:T(8,128)(2,1)S(1)}, bf16[1024,1024]{1,0:T(8,128)(2,1)S(1)}, u32[]{:S(2)}, u32[]{:S(2)}) collective-permute-start(bf16[1024,1024]{1,0:T(8,128)(2,1)S(1)} %convert_element_type.343), channel_id=1, source_target_pairs={{0,8},{8,16},{16,24},{1,9},{9,17},{17,25},{2,10},{10,18},{18,26},{... | collective-permute-start | bytes 6291464 | tf_op jit(solution)/shard_map/ppermute | solution.py:18
  539.1 82.8 %collective-permute-start.2 = (bf16[2,256,1024]{2,1,0:T(8,128)(2,1)}, bf16[2,256,1024]{2,1,0:T(8,128)(2,1)}, u32[]{:S(2)}, u32[]{:S(2)}) collective-permute-start(bf16[2,256,1024]{2,1,0:T(8,128)(2,1)} %collective-permute-done.1), channel_id=1, source_target_pairs={{0,8},{8,16},{16,24},{1,9},{9,17},{17,25},{2,10},{10,18},{18,26},{... | collective-permute-start | bytes 3145736 | tf_op jit(solution)/shard_map/ppermute | solution.py:18
  581.3 51.7 %collective-permute-start.10 = (bf16[1024,1024]{1,0:T(8,128)(2,1)}, bf16[1024,1024]{1,0:T(8,128)(2,1)}, u32[]{:S(2)}, u32[]{:S(2)}) collective-permute-start(bf16[1024,1024]{1,0:T(8,128)(2,1)} %convert_element_type.358), channel_id=1, source_target_pairs={{0,8},{8,16},{16,24},{1,9},{9,17},{17,25},{2,10},{10,18},{18,26},{... | collective-permute-start | bytes 6291464 | tf_op jit(solution)/shard_map/ppermute | solution.py:18
  620.2 27.6 collective-permute-start.7
  683.7 171.7 %collective-permute-start.14 = (bf16[1024,1024]{1,0:T(8,128)(2,1)}, bf16[1024,1024]{1,0:T(8,128)(2,1)}, u32[]{:S(2)}, u32[]{:S(2)}) collective-permute-start(bf16[1024,1024]{1,0:T(8,128)(2,1)} %convert_element_type.367), channel_id=1, source_target_pairs={{0,8},{8,16},{16,24},{1,9},{9,17},{17,25},{2,10},{10,18},{18,26},{... | collective-permute-start | bytes 6291464 | tf_op jit(solution)/shard_map/ppermute | solution.py:18
  743.5 117.9 %collective-permute-start.13 = (bf16[1024,1024]{1,0:T(8,128)(2,1)}, bf16[1024,1024]{1,0:T(8,128)(2,1)}, u32[]{:S(2)}, u32[]{:S(2)}) collective-permute-start(bf16[1024,1024]{1,0:T(8,128)(2,1)} %convert_element_type.365), channel_id=1, source_target_pairs={{0,8},{8,16},{16,24},{1,9},{9,17},{17,25},{2,10},{10,18},{18,26},{... | collective-permute-start | bytes 6291464 | tf_op jit(solution)/shard_map/ppermute | solution.py:18
  847.3 25.8 collective-permute-start.11
  936.4 1649.8 %reduce-scatter.43.cloned.1.call-start = ((), (), s32[]{:S(2)}) async-start(), calls=%async_computation.38 | async-start | bytes 540672
  952.5 1683.1 %reduce-scatter.25.cloned.1.call-start = ((), (), s32[]{:S(2)}) async-start(), calls=%async_computation.29 | async-start | bytes 4325376 | tf_op jit(solution)/shard_map/reduce_scatter | solution.py:418
  956.6 1679.1 %reduce-scatter.19.cloned.1.call-start = ((), (), s32[]{:S(2)}) async-start(), calls=%async_computation.26 | async-start | bytes 4325376 | tf_op jit(solution)/shard_map/reduce_scatter | solution.py:413
  964.1 1671.6 %reduce-scatter.21.cloned.1.call-start = ((), (), s32[]{:S(2)}) async-start(), calls=%async_computation.27 | async-start | bytes 4325376 | tf_op jit(solution)/shard_map/reduce_scatter | solution.py:414
  972.9 45.8 %collective-permute-start.15 = (bf16[2,256,1024]{1,2,0:T(8,128)(2,1)}, bf16[2,256,1024]{1,2,0:T(8,128)(2,1)}, u32[]{:S(2)}, u32[]{:S(2)}) collective-permute-start(bf16[2,256,1024]{1,2,0:T(8,128)(2,1)} %pad_maximum_fusion.1), channel_id=1, source_target_pairs={{8,0},{16,8},{24,16},{9,1},{17,9},{25,17},{10,2},{18,10},{26,18},{... | collective-permute-start | bytes 3145736 | tf_op jit(solution)/shard_map/ppermute | solution.py:18
  1042.3 38.0 collective-permute-start.17
  1086.2 1549.4 %reduce-scatter.23.cloned.1.call-start = ((), (), s32[]{:S(2)}) async-start(), calls=%async_computation.28 | async-start | bytes 4325376 | tf_op jit(solution)/shard_map/reduce_scatter | solution.py:415
  1128.5 1545.2 %reduce-scatter.33.cloned.1.call-start = ((), (), s32[]{:S(2)}) async-start(), calls=%async_computation.33 | async-start | bytes 4325376 | tf_op jit(solution)/shard_map/reduce_scatter | solution.py:422
  1170.9 79.5 %collective-permute-start.25 = (bf16[1024,1024]{1,0:T(8,128)(2,1)S(1)}, bf16[1024,1024]{1,0:T(8,128)(2,1)S(1)}, u32[]{:S(2)}, u32[]{:S(2)}) collective-permute-start(bf16[1024,1024]{1,0:T(8,128)(2,1)S(1)} %convert_element_type.409), channel_id=1, source_target_pairs={{8,0},{16,8},{24,16},{9,1},{17,9},{25,17},{10,2},{18,10},{26,18},{... | collective-permute-start | bytes 6291464 | tf_op jit(solution)/shard_map/ppermute | solution.py:18
  1172.8 82.2 %collective-permute-start.24 = (bf16[1024,1024]{1,0:T(8,128)(2,1)S(1)}, bf16[1024,1024]{1,0:T(8,128)(2,1)S(1)}, u32[]{:S(2)}, u32[]{:S(2)}) collective-permute-start(bf16[1024,1024]{1,0:T(8,128)(2,1)S(1)} %convert_element_type.407), channel_id=1, source_target_pairs={{8,0},{16,8},{24,16},{9,1},{17,9},{25,17},{10,2},{18,10},{26,18},{... | collective-permute-start | bytes 6291464 | tf_op jit(solution)/shard_map/ppermute | solution.py:18
  1174.7 84.9 %collective-permute-start.23 = (bf16[1024,1024]{1,0:T(8,128)(2,1)S(1)}, bf16[1024,1024]{1,0:T(8,128)(2,1)S(1)}, u32[]{:S(2)}, u32[]{:S(2)}) collective-permute-start(bf16[1024,1024]{1,0:T(8,128)(2,1)S(1)} %convert_element_type.405), channel_id=1, source_target_pairs={{8,0},{16,8},{24,16},{9,1},{17,9},{25,17},{10,2},{18,10},{26,18},{... | collective-permute-start | bytes 6291464 | tf_op jit(solution)/shard_map/ppermute | solution.py:18
  1176.4 87.9 %collective-permute-start.22 = (bf16[1024,1024]{1,0:T(8,128)(2,1)S(1)}, bf16[1024,1024]{1,0:T(8,128)(2,1)S(1)}, u32[]{:S(2)}, u32[]{:S(2)}) collective-permute-start(bf16[1024,1024]{1,0:T(8,128)(2,1)S(1)} %convert_element_type.403), channel_id=1, source_target_pairs={{8,0},{16,8},{24,16},{9,1},{17,9},{25,17},{10,2},{18,10},{26,18},{... | collective-permute-start | bytes 6291464 | tf_op jit(solution)/shard_map/ppermute | solution.py:18
  1292.4 897.9 %collective-permute-start.29 = (bf16[1024,1024]{1,0:T(8,128)(2,1)S(1)}, bf16[1024,1024]{1,0:T(8,128)(2,1)S(1)}, u32[]{:S(2)}, u32[]{:S(2)}) collective-permute-start(bf16[1024,1024]{1,0:T(8,128)(2,1)S(1)} %convert_element_type.417), channel_id=1, source_target_pairs={{8,0},{16,8},{24,16},{9,1},{17,9},{25,17},{10,2},{18,10},{26,18},{... | collective-permute-start | bytes 6291464 | tf_op jit(solution)/shard_map/ppermute | solution.py:18
  1296.3 898.5 %collective-permute-start.28 = (bf16[1024,1024]{1,0:T(8,128)(2,1)S(1)}, bf16[1024,1024]{1,0:T(8,128)(2,1)S(1)}, u32[]{:S(2)}, u32[]{:S(2)}) collective-permute-start(bf16[1024,1024]{1,0:T(8,128)(2,1)S(1)} %convert_element_type.415), channel_id=1, source_target_pairs={{8,0},{16,8},{24,16},{9,1},{17,9},{25,17},{10,2},{18,10},{26,18},{... | collective-permute-start | bytes 6291464 | tf_op jit(solution)/shard_map/ppermute | solution.py:18
  1297.6 900.2 %collective-permute-start.27 = (bf16[1024,1024]{1,0:T(8,128)(2,1)S(1)}, bf16[1024,1024]{1,0:T(8,128)(2,1)S(1)}, u32[]{:S(2)}, u32[]{:S(2)}) collective-permute-start(bf16[1024,1024]{1,0:T(8,128)(2,1)S(1)} %convert_element_type.413), channel_id=1, source_target_pairs={{8,0},{16,8},{24,16},{9,1},{17,9},{25,17},{10,2},{18,10},{26,18},{... | collective-permute-start | bytes 6291464 | tf_op jit(solution)/shard_map/ppermute | solution.py:18
  1301.4 899.8 %collective-permute-start.26 = (bf16[1024,1024]{1,0:T(8,128)(2,1)S(1)}, bf16[1024,1024]{1,0:T(8,128)(2,1)S(1)}, u32[]{:S(2)}, u32[]{:S(2)}) collective-permute-start(bf16[1024,1024]{1,0:T(8,128)(2,1)S(1)} %convert_element_type.411), channel_id=1, source_target_pairs={{8,0},{16,8},{24,16},{9,1},{17,9},{25,17},{10,2},{18,10},{26,18},{... | collective-permute-start | bytes 6291464 | tf_op jit(solution)/shard_map/ppermute | solution.py:18
  2533.8 282.5 %reduce-scatter.35.cloned.1.call-start = ((), (), s32[]{:S(2)}) async-start(), calls=%async_computation.34 | async-start | bytes 4325376 | tf_op jit(solution)/shard_map/reduce_scatter | solution.py:423
  2534.3 426.1 %reduce-scatter.31.cloned.1.call-start = ((), (), s32[]{:S(2)}) async-start(), calls=%async_computation.32 | async-start | bytes 4325376 | tf_op jit(solution)/shard_map/reduce_scatter | solution.py:421
  2539.9 564.4 %reduce-scatter.29.cloned.1.call-start = ((), (), s32[]{:S(2)}) async-start(), calls=%async_computation.31 | async-start | bytes 4325376 | tf_op jit(solution)/shard_map/reduce_scatter | solution.py:420
  2546.1 701.8 %reduce-scatter.27.cloned.1.call-start = ((), (), s32[]{:S(2)}) async-start(), calls=%async_computation.30 | async-start | bytes 4325376 | tf_op jit(solution)/shard_map/reduce_scatter | solution.py:419
  2552.3 945.1 %reduce-scatter.41.cloned.1.call-start = ((), (), s32[]{:S(2)}) async-start(), calls=%async_computation.37 | async-start | bytes 11894784 | tf_op jit(solution)/shard_map/reduce_scatter | solution.py:301
  2559.8 1190.3 %reduce-scatter.39.cloned.1.call-start = ((), (), s32[]{:S(2)}) async-start(), calls=%async_computation.36 | async-start | bytes 11894784 | tf_op jit(solution)/shard_map/reduce_scatter | solution.py:300
  2567.4 1432.9 %reduce-scatter.37.cloned.1.call-start = ((), (), s32[]{:S(2)}) async-start(), calls=%async_computation.35 | async-start | bytes 11894784 | tf_op jit(solution)/shard_map/reduce_scatter | solution.py:299
  (125 other events, 3891.6 us)
Sparse Core Ops, SparseCore 0:
  10.2 51.9 all-gather.16
  64.3 47.7 all-gather.14
  114.3 47.7 all-gather.22
  164.0 47.7 all-gather.20
  213.8 47.7 all-gather.24
  263.6 47.7 all-gather.26
  313.6 47.7 all-gather.28
  363.5 47.7 all-gather.18
  413.5 48.2 all-gather.30
  463.8 91.6 all-gather.34
  557.7 90.4 all-gather.32
  650.2 90.8 all-gather.36
  936.5 208.2 reduce-scatter.44
  1146.9 131.0 reduce-scatter.42
  1280.7 140.4 reduce-scatter.24
  1423.9 141.0 reduce-scatter.18
  1567.7 141.5 reduce-scatter.20
  1712.0 141.8 reduce-scatter.22
  2533.9 139.7 reduce-scatter.32
  2676.4 139.8 reduce-scatter.34
  2819.1 141.2 reduce-scatter.30
  2963.3 140.9 reduce-scatter.28
  3107.1 140.7 reduce-scatter.26
  3250.6 246.7 reduce-scatter.40
  3500.3 249.7 reduce-scatter.38
  3752.8 247.4 reduce-scatter.36
where the time goes:
time: 4020 us; the launch traced here: 4010 us
  waiting for transfers between devices  2720 us (68%)
  matrix products  427 us (11%)
  other arithmetic  261 us (6%)
  starting transfers between devices  216 us (5%)
  local copies, waits for them, and re-layouts  185 us (5%)
  blocking collectives  133 us (3%)
  loops' own time  50.3 us (1%)
    ppermute x30, waiting for transfers between devices, from_behind(): lax.ppermute(value, axis, [(source, source + steps) for source in range(f...  1040 us
    dot_general x60, matrix products, matmul(): return jnp.dot(left, right, precision=highest)  306 us
    reduce_scatter x1, waiting for transfers between devices, on_device(): lax.psum_scatter(grad_upper, ('ctx', 'shard'), scatter_dimension=0, tiled...  253 us
    reduce_scatter x1, waiting for transfers between devices, on_device(): lax.psum_scatter(grad_gate, ('ctx', 'shard'), scatter_dimension=0, tiled=...  250 us
    reduce_scatter x1, waiting for transfers between devices, on_device(): lax.psum_scatter(grad_down, ('ctx', 'shard'), scatter_dimension=0, tiled=...  250 us
    ppermute x30, starting transfers between devices, from_behind(): lax.ppermute(value, axis, [(source, source + steps) for source in range(f...  215 us
    reduce_scatter x1, waiting for transfers between devices, on_device(): lax.psum_scatter(grad_mvalue, ('ctx', 'shard'), scatter_dimension=0, tile...  144 us
    reduce_scatter x1, waiting for transfers between devices, on_device(): lax.psum_scatter(grad_mkey, ('ctx', 'shard'), scatter_dimension=0, tiled=...  144 us
  transfers between devices with their start and end apart: 56, of which 26 were waited for; matrix products, arithmetic and copies ran while one was open for 21% of the time, Pallas kernels for 0%

commit v1 on v0

v1 whole, which is shorter than its diff:
```python
import jax
import jax.numpy as jnp
from jax import lax
from jax.sharding import PartitionSpec as P

HEADS = 8
HEAD_DIM = 128
WINDOW = 1024
SPAN = 128
EPS = 1e-05
bf16 = jnp.bfloat16
f32 = jnp.float32


def split_axis(size, inner):
    return size // inner, inner


def shard_inner(size):
    inner = 1
    while inner * inner * 4 <= size:
        inner *= 2
    return inner


def dot(left, right):
    return jnp.dot(left, right, preferred_element_type=f32)


def dot_t(left, right):
    return lax.dot_general(left, right, (((1,), (1,)), ((), ())), preferred_element_type=f32)


def t_dot(left, right):
    return lax.dot_general(left, right, (((0,), (0,)), ((), ())), preferred_element_type=f32)


def line_place(axis, stride, count):
    return (lax.axis_index(axis) // stride) % count


def shift(value, axis, stride, count, step):
    size = lax.axis_size(axis)
    pairs = [
        (i, i + step * stride) for i in range(size) if 0 <= (i // stride) % count + step < count
    ]
    return lax.ppermute(value, axis, pairs)


def swap(value, axis, stride):
    size = lax.axis_size(axis)
    return lax.ppermute(value, axis, [(i, i ^ stride) for i in range(size)])


def line_gather(value, axis, stride, count):
    if count == 1:
        return value[None]
    place = line_place(axis, stride, count)
    if count == 2:
        other = swap(value, axis, stride)
        return jnp.stack([jnp.where(place == 0, value, other), jnp.where(place == 0, other, value)])
    below, above = [], []
    low = high = value
    for _ in range(count - 1):
        low = shift(low, axis, stride, count, 1)
        high = shift(high, axis, stride, count, -1)
        below.append(low)
        above.append(high)
    every = jnp.stack(below[::-1] + [value] + above)
    return lax.dynamic_slice_in_dim(every, count - 1 - place, count, 0)


def line_reduce(blocks, axis, stride, count):
    if count == 1:
        return blocks[0]
    place = line_place(axis, stride, count)

    def own(index):
        return lax.dynamic_index_in_dim(blocks, index, 0, keepdims=False)

    if count == 2:
        return own(place) + swap(own(1 - place).astype(bf16), axis, stride).astype(f32)
    right = left = None
    for step in range(1, count):
        send_right = own(jnp.clip(place + count - step, 0, count - 1))
        send_left = own(jnp.clip(place - count + step, 0, count - 1))
        if right is not None:
            send_right = send_right + right.astype(f32)
            send_left = send_left + left.astype(f32)
        right = shift(send_right.astype(bf16), axis, stride, count, 1)
        left = shift(send_left.astype(bf16), axis, stride, count, -1)
    return own(place) + right.astype(f32) + left.astype(f32)


def gather_ctx(value):
    size = lax.axis_size("ctx")
    outer, inner = split_axis(size, 2 if size % 2 == 0 else 1)
    columns = line_gather(value, "ctx", inner, outer)
    both = line_gather(columns, "ctx", 1, inner)
    both = jnp.swapaxes(both, 0, 1)
    return both.reshape((size * value.shape[0],) + value.shape[1:])


def reduce_ctx(value):
    size = lax.axis_size("ctx")
    outer, inner = split_axis(size, 2 if size % 2 == 0 else 1)
    blocks = value.reshape((outer, inner, value.shape[0] // size) + value.shape[1:])
    kept = line_reduce(jnp.swapaxes(blocks, 0, 1), "ctx", 1, inner)
    return line_reduce(kept, "ctx", inner, outer)


def gather_shard(value):
    size = lax.axis_size("shard")
    outer, inner = split_axis(size, shard_inner(size))
    columns = line_gather(value, "shard", inner, outer)
    both = line_gather(columns, "shard", 1, inner)
    both = jnp.swapaxes(both, 0, 1)
    return both.reshape((size,) + value.shape)


def reduce_shard(value):
    size = lax.axis_size("shard")
    outer, inner = split_axis(size, shard_inner(size))
    blocks = value.reshape((outer, inner) + value.shape[1:])
    kept = line_reduce(jnp.swapaxes(blocks, 0, 1), "shard", 1, inner)
    return line_reduce(kept, "shard", inner, outer)


def rms_rows(values):
    return lax.rsqrt(jnp.mean(values * values, axis=-1, keepdims=True) + EPS)


def rms_back(values, root, gain, grad):
    scaled = grad * gain
    mean = jnp.mean(values * scaled, axis=-1, keepdims=True)
    return root * scaled - values * (root * root * root * mean), jnp.sum(grad * values * root, axis=0)


def silu_parts(z):
    s = jax.nn.sigmoid(z)
    slope = s * (1.0 + z * (1.0 - s))
    bend = s * (1.0 - s) * (2.0 + z * (1.0 - 2.0 * s))
    return z * s, slope, bend


def tables(keep, momentum, rate):
    count = keep.shape[0]
    a = jnp.ones((), f32)
    b = jnp.zeros((count,), f32)
    m = jnp.zeros((count,), f32)
    spot = jnp.arange(count)
    all_a, all_b = [], []
    for c in range(count):
        all_a.append(a)
        all_b.append(b)
        m = momentum[c] * m + jnp.where(spot == c, rate[c], 0.0)
        b = keep[c] * b + m
        a = keep[c] * a
    return jnp.stack(all_a), jnp.stack(all_b)


def on_device(
    block_input, lengths, mem_keep, mem_momentum, mem_rate, norm_gain, w_query, w_key, w_value,
    persist_keys, persist_values, w_out, mem_query, mem_key, mem_value, mem_first, mem_second,
    ffn_gain, w_gate, w_up, w_down, cotangent,
):
    ctx = lax.axis_size("ctx")
    shard = lax.axis_size("shard")
    me = lax.axis_index("ctx")
    rows, width = block_input.shape[1:]
    total = rows * ctx
    part = width // ctx
    hidden = w_gate.shape[1]
    wrows = w_query.shape[0]
    drows = w_down.shape[0]
    dpart = drows // ctx
    fpart = dpart * shard
    heads = HEADS // ctx
    persist = persist_keys.shape[0]
    chunks = total // SPAN

    def mine(w, size):
        return lax.dynamic_slice_in_dim(w, me * size, size, 1)

    def mine_ffn(w):
        return lax.dynamic_index_in_dim(w.reshape(w.shape[0], shard, ctx, dpart), me, 2, keepdims=False).reshape(w.shape[0], fpart)

    def full_weights(group):
        local = jnp.concatenate(group, axis=1)
        quarter = lax.dynamic_slice_in_dim(local, me * (wrows // ctx), wrows // ctx, 0)
        got = gather_shard(quarter).reshape(shard * (wrows // ctx), -1)
        got = gather_ctx(got).reshape(ctx, shard, wrows // ctx, -1)
        got = jnp.swapaxes(got, 0, 1).reshape(shard * wrows, -1)
        return [got[:, k * width : (k + 1) * width] for k in range(len(group))]

    small = jnp.concatenate([persist_keys, persist_values, norm_gain[None], ffn_gain[None]], 0)
    small = jnp.swapaxes(gather_shard(small), 0, 1).reshape(2 * persist + 2, width)
    p_keys = mine(small[:persist], part)
    p_values = mine(small[persist : 2 * persist], part)
    gain_one = small[2 * persist].astype(f32)[None]
    gain_two = small[2 * persist + 1].astype(f32)[None]

    scalars = jnp.concatenate([mem_keep, mem_momentum, mem_rate], 0).T
    scalars = gather_ctx(scalars)
    a_tab, b_tab = tables(scalars[:, 0], scalars[:, 1], scalars[:, 2])
    tokens_low = gather_ctx(block_input[0])
    mk_w, first_w = full_weights([mem_key, mem_first])
    mv_w, second_w = full_weights([mem_value, mem_second])
    qkv = gather_shard(jnp.concatenate([mine(w_query, part), mine(w_key, part), mine(w_value, part)], 1)).reshape(width, 3 * part)
    mq_w, out_w = full_weights([mem_query, w_out])
    gateup = gather_shard(jnp.concatenate([mine_ffn(w_gate), mine_ffn(w_up)], 1)).reshape(width, 2 * fpart)
    down = gather_shard(lax.dynamic_slice_in_dim(w_down, me * dpart, dpart, 0)).reshape(fpart, width)
    cot_low = gather_ctx(cotangent[0])

    length = lengths[0]
    slots = jnp.arange(total, dtype=jnp.int32)
    alive = (slots < length).astype(f32)[:, None]
    tokens = tokens_low.astype(f32)
    root_one = rms_rows(tokens)
    normed = (tokens * root_one * gain_one).astype(bf16)
    mkey = dot(normed, mk_w).astype(bf16)
    mvalue = dot(normed, mv_w).astype(bf16)
    mquery = dot(normed, mq_w).astype(bf16)
    a_rows = jnp.repeat(a_tab, SPAN)[:, None]
    b_all = jnp.repeat(jnp.repeat(b_tab, SPAN, axis=0), SPAN, axis=1)

    qkv_rows = dot(normed, qkv).astype(bf16)
    q = qkv_rows[:, :part].reshape(total, heads, HEAD_DIM)
    k = jnp.concatenate([p_keys, qkv_rows[:, part : 2 * part]], 0).reshape(-1, heads, HEAD_DIM)
    v = jnp.concatenate([p_values, qkv_rows[:, 2 * part :]], 0).reshape(-1, heads, HEAD_DIM)
    scale = HEAD_DIM ** (-0.5)
    window_ok = (slots[None, :] <= slots[:, None]) & (slots[:, None] - slots[None, :] < WINDOW) & (slots[None, :] < length)
    allowed = jnp.concatenate([jnp.ones((total, persist), dtype=bool), window_ok], 1)
    scores = jnp.einsum("thd,shd->hts", q, k, preferred_element_type=f32) * scale
    scores = jnp.where(allowed[None], scores, -1e30)
    peak = jnp.max(scores, axis=-1, keepdims=True)
    expo = jnp.exp(scores - peak)
    probs_f = expo / jnp.sum(expo, axis=-1, keepdims=True)
    probs = probs_f.astype(bf16)
    attended_mine = jnp.einsum("hts,shd->thd", probs, v, preferred_element_type=f32).reshape(total, part)
    att = gather_ctx(attended_mine.astype(bf16)[None]).swapaxes(0, 1).reshape(total, width).astype(f32)

    def blk(arr, c):
        return arr[c * SPAN : (c + 1) * SPAN]

    key_first = dot(mkey, first_w)
    kk = b_all * dot_t(mkey, mkey)
    kk = kk.astype(bf16)
    z_l, h_l, e_l, u_l, g_l = [], [], [], [], []
    hcat = ecat = gcat = None
    for c in range(chunks):
        z = a_tab[c] * blk(key_first, c)
        if c:
            z = z - dot(blk(kk, c)[:, : c * SPAN], gcat)
        h, slope, _ = silu_parts(z)
        hb = h.astype(bf16)
        pred = a_tab[c] * dot(hb, second_w)
        if c:
            bc = blk(b_all, c)[:, : c * SPAN]
            pred = pred - dot((bc * dot_t(hb, hcat)).astype(bf16), ecat)
        err = blk(alive, c) * (pred - blk(mvalue, c).astype(f32)) / SPAN
        eb = err.astype(bf16)
        u = a_tab[c] * dot_t(eb, second_w)
        if c:
            u = u - dot((bc * dot_t(eb, ecat)).astype(bf16), hcat)
        gb = (u * slope).astype(bf16)
        hcat = hb if c == 0 else jnp.concatenate([hcat, hb], 0)
        ecat = eb if c == 0 else jnp.concatenate([ecat, eb], 0)
        gcat = gb if c == 0 else jnp.concatenate([gcat, gb], 0)
        z_l.append(z)
        u_l.append(u)
    kq = (b_all * dot_t(mquery, mkey)).astype(bf16)
    zq = a_rows * dot(mquery, first_w) - dot(kq, gcat)
    hq, slope_q, _ = silu_parts(zq)
    hqb = hq.astype(bf16)
    hqh = (b_all * dot_t(hqb, hcat)).astype(bf16)
    recalled = a_rows * dot(hqb, second_w) - dot(hqh, ecat)

    combined = (att * recalled).astype(bf16)
    middle = tokens + dot(combined, out_w)
    root_two = rms_rows(middle)
    normed_two = (middle * root_two * gain_two).astype(bf16)
    gu = dot(normed_two, gateup)
    gate, up = gu[:, :fpart], gu[:, fpart:]
    act, gate_slope, _ = silu_parts(gate)
    activated = (act * up).astype(bf16)
    ffn_own = reduce_ctx(dot(activated, down))
    mid_own = lax.dynamic_slice_in_dim(middle, me * rows, rows, 0)
    alive_own = lax.dynamic_slice_in_dim(alive, me * rows, rows, 0)
    result = alive_own * (mid_own + ffn_own)

    d_ffn = (cot_low.astype(f32) * alive).astype(bf16)
    d_result = d_ffn.astype(f32)
    g_down = t_dot(activated, d_ffn)
    d_act = dot_t(d_ffn, down)
    d_gate = (d_act * up * gate_slope).astype(bf16)
    d_up = (d_act * act).astype(bf16)
    d_gu = jnp.concatenate([d_gate, d_up], 1)
    g_gu = t_dot(normed_two, d_gu)
    d_normed_two = gather_ctx(reduce_ctx(dot_t(d_gu, gateup)).astype(bf16)).astype(f32)
    d_norm, g_gain_two = rms_back(middle, root_two, gain_two, d_normed_two)
    d_middle = d_result + d_norm
    d_branch = d_middle.astype(bf16)
    g_out = t_dot(mine(combined, part), d_branch)
    d_combined = dot_t(d_branch, out_w)
    d_att = (mine(d_combined, part) * mine(recalled, part)).astype(bf16)
    d_rec = (d_combined * att).astype(bf16)

    d_heads = d_att.reshape(total, heads, HEAD_DIM)
    d_probs = jnp.einsum("thd,shd->hts", d_heads, v, preferred_element_type=f32)
    centre = jnp.sum(d_probs * probs_f, axis=-1, keepdims=True)
    d_scores = (probs_f * (d_probs - centre)).astype(bf16)
    d_q = (scale * jnp.einsum("hts,shd->thd", d_scores, k, preferred_element_type=f32)).reshape(total, part)
    d_k = (scale * jnp.einsum("hts,thd->shd", d_scores, q, preferred_element_type=f32)).reshape(-1, part)
    d_v = jnp.einsum("hts,thd->shd", probs, d_heads, preferred_element_type=f32).reshape(-1, part)
    g_pkeys, g_pvalues = d_k[:persist], d_v[:persist]
    d_qkv = jnp.concatenate([d_q, d_k[persist:], d_v[persist:]], 1).astype(bf16)
    g_qkv = t_dot(normed, d_qkv)
    d_normed_qkv = reduce_ctx(dot_t(d_qkv, qkv))

    dh_q = a_rows * dot_t(d_rec, second_w)
    n1 = (b_all * dot_t(d_rec, ecat)).astype(bf16)
    dh_q = dh_q - dot(n1, hcat)
    dz_q = (dh_q * slope_q).astype(bf16)
    d_e = -t_dot(hqh, d_rec)
    d_h = -t_dot(n1, hqb)
    d_g = -t_dot(kq, dz_q)
    n2 = (b_all * dot_t(dz_q, gcat)).astype(bf16)
    d_mq = a_rows * dot_t(dz_q, first_w) - dot(n2, mkey)
    d_mk = -t_dot(n2, mquery)
    dz_l, du_l, dp_l = [None] * chunks, [None] * chunks, [None] * chunks
    for c in range(chunks - 1, -1, -1):
        lo = c * SPAN
        z, u = z_l[c], u_l[c]
        _, slope, bend = silu_parts(z)
        hb, eb = blk(hcat, c), blk(ecat, c)
        dg = blk(d_g, c)
        du = dg * slope
        dz = dg * u * bend
        dub = du.astype(bf16)
        de = blk(d_e, c) + a_tab[c] * dot(dub, second_w)
        if c:
            bc = blk(b_all, c)[:, :lo]
            hl, el = hcat[:lo], ecat[:lo]
            n3 = (bc * dot_t(dub, hl)).astype(bf16)
            m3 = (bc * dot_t(eb, el)).astype(bf16)
            de = de - dot(n3, el)
        dp = blk(alive, c) * de / SPAN
        dpb = dp.astype(bf16)
        dh = blk(d_h, c) + a_tab[c] * dot_t(dpb, second_w)
        if c:
            n4 = (bc * dot_t(dpb, el)).astype(bf16)
            m4 = (bc * dot_t(hb, hl)).astype(bf16)
            dh = dh - dot(n4, hl)
        dz = dz + dh * slope
        dzb = dz.astype(bf16)
        if c:
            m5 = blk(kk, c)[:, :lo]
            d_h = d_h[:lo] - t_dot(jnp.concatenate([m3, n4], 0), jnp.concatenate([dub, hb], 0))
            d_e = d_e[:lo] - t_dot(jnp.concatenate([n3, m4], 0), jnp.concatenate([eb, dpb], 0))
            d_g = d_g[:lo] - t_dot(m5, dzb)
        dz_l[c], du_l[c], dp_l[c] = dzb, dub, dp
    dz = jnp.concatenate(dz_l, 0)
    du = jnp.concatenate(du_l, 0)
    dp = jnp.concatenate(dp_l, 0)
    d_mv = (-dp).astype(bf16)
    n5 = (b_all * dot_t(dz, gcat)).astype(bf16)
    d_mk = d_mk + a_rows * dot_t(dz, first_w) - dot(n5, mkey) - t_dot(n5, mkey)
    d_mk = d_mk.astype(bf16)
    d_mq = d_mq.astype(bf16)

    def scaled(arr):
        return (a_rows * arr.astype(f32)).astype(bf16)

    g_first = t_dot(mine(mkey, part), scaled(dz)) + t_dot(mine(mquery, part), scaled(dz_q))
    g_second = t_dot(mine(hcat, part), scaled(dp)) + t_dot(mine(hqb, part), scaled(d_rec)) + t_dot(mine(du, part), scaled(ecat))
    normed_mine = mine(normed, part)
    g_mq = t_dot(normed_mine, d_mq)
    g_mk = t_dot(normed_mine, d_mk)
    g_mv = t_dot(normed_mine, d_mv)

    def own(arr):
        return lax.dynamic_slice_in_dim(arr, me * rows, rows, 0)

    d_normed = d_normed_qkv + dot_t(own(d_mq), mq_w) + dot_t(own(d_mk), mk_w) + dot_t(own(d_mv), mv_w)
    d_tok, g_gain_one = rms_back(own(tokens), own(root_one), gain_one, d_normed)
    input_grad = own(d_middle) + d_tok

    each = width // (ctx * shard)
    by_rows = jnp.concatenate([g_out, g_mq, g_mk, g_mv, g_first, g_second], 1)
    by_rows = reduce_shard(by_rows.reshape(shard, each, -1))
    by_rows = [by_rows[:, i * width : (i + 1) * width] for i in range(6)]
    columns = jnp.concatenate([g_qkv, g_gu], 1).reshape(ctx, shard, each, -1)
    columns = reduce_shard(jnp.swapaxes(columns, 0, 1))
    columns = lax.all_to_all(columns, "ctx", 0, 0)
    g_q, g_k, g_v = [
        jnp.swapaxes(columns[:, :, i * part : (i + 1) * part], 0, 1).reshape(each, width) for i in range(3)
    ]

    def ffn_columns(begin):
        taken = columns[:, :, begin : begin + fpart].reshape(ctx, each, shard, dpart)
        return jnp.transpose(taken, (1, 2, 0, 3)).reshape(each, hidden)

    g_gate = ffn_columns(3 * part)
    g_up = ffn_columns(3 * part + fpart)
    g_down = reduce_shard(g_down.reshape(shard, dpart, width))
    pairs = []
    for i in range(ctx):
        for s in range(shard):
            pairs.append((i * shard + s, s * ctx + i))
    g_down = lax.ppermute(g_down, ("ctx", "shard"), pairs)

    def narrow(arr):
        return jnp.swapaxes(arr.reshape(arr.shape[0], shard, each), 0, 1)

    gain_one_all = lax.psum(g_gain_one, ("ctx", "shard"))
    tiny = jnp.concatenate([g_pkeys, g_pvalues, mine(g_gain_two[None], part)], 0)
    tiny = lax.psum(tiny, "shard")
    s_me = lax.axis_index("shard")
    tiny = lax.dynamic_slice_in_dim(tiny, s_me * each, each, 1)
    gain_one_out = lax.dynamic_slice_in_dim(gain_one_all, (me * shard + s_me) * each, each, 0)
    return (
        result.astype(bf16)[None],
        input_grad.astype(bf16)[None],
        gain_one_out,
        g_q, g_k, g_v,
        tiny[:persist], tiny[persist : 2 * persist],
        by_rows[0], by_rows[1], by_rows[2], by_rows[3], by_rows[4], by_rows[5],
        tiny[2 * persist],
        g_gate, g_up, g_down,
    )


def solution(mesh):
    row = P("shard", None)
    col = P(None, "shard")
    vec = P("shard")
    seq = P("shard", "ctx", None)
    sc = P("shard", "ctx")
    in_specs = (
        seq, vec, sc, sc, sc, vec, row, row, row, col, col, row, row, row, row, row, row, vec, row, row, row, seq,
    )
    both = ("ctx", "shard")
    orow = P(both, None)
    out_specs = (
        seq, seq, P(both), orow, orow, orow, P(None, both), P(None, both), orow, orow, orow, orow, orow, orow,
        P(both), orow, orow, orow,
    )
    return jax.shard_map(on_device, mesh=mesh, in_specs=in_specs, out_specs=out_specs, check_vma=False)
```

time: 4020 us -> 1080 us (0.27)
  waiting for transfers between devices: 2720 us -> 175 us
  matrix products: 427 us -> 277 us
  other arithmetic: 261 us -> 127 us
  loops' own time: 50.3 us -> 0 us
    reduce_scatter x12 -> x0, waiting for transfers between devices: 1360 us -> none  [the longest x1 253 us: on_device(): lax.psum_scatter(grad_upper, ('ctx', 'shard'), scatter_dimension=0, tiled...]
    ppermute x30 -> x93, waiting for transfers between devices: 1040 us -> 162 us  [the longest x60 86.5 us: shift(): return lax.ppermute(value, axis, pairs)]
    all_gather x12 -> x0, waiting for transfers between devices: 302 us -> none  [the longest x1 47.6 us: on_device(): lax.all_gather(mem_value, 'shard', axis=0, tiled=True)]
    dot_general x96 -> x169, matrix products: 427 us -> 270 us  [the longest x60 98.1 us: dot_t(): lax.dot_general(left, right, (((1,), (1,)), ((), ())), preferred_element_...]
    psum x0 -> x2, blocking collectives: none -> 113 us  [the longest x1 75.1 us: on_device(): tiny = lax.psum(tiny, 'shard')]
    select_n x22 -> x1, other arithmetic: 111 us -> 0.01 us  [line_gather(): jnp.where(place == 0, value, other)]
    all_gather x4 -> x0, blocking collectives: 93.5 us -> none  [the longest x1 26.5 us: on_device(): lax.all_gather(persist_keys, 'shard', axis=1, tiled=True)]
    convert_element_type x41 -> x28, other arithmetic: 116 us -> 33.9 us  [the longest x6 8.35 us: line_reduce(): right = shift(send_right.astype(bf16), axis, stride, count, 1)]
  transfers between devices with their start and end apart: 56 -> 94, of which waited for: 26 -> 32; matrix products, arithmetic and copies ran while one was open for 21% -> 27% of each run, Pallas kernels for 0% -> 0%
where the time goes in v1:
time: 1080 us; the launch traced here: 1070 us
  matrix products  277 us (26%)
  starting transfers between devices  192 us (18%)
  waiting for transfers between devices  175 us (16%)
  local copies, waits for them, and re-layouts  168 us (16%)
  other arithmetic  127 us (12%)
  blocking collectives  113 us (10%)
  between operations  13.6 us (1%)
    ppermute x60, starting transfers between devices, shift(): return lax.ppermute(value, axis, pairs)  161 us
    dot_general x60, matrix products, dot_t(): lax.dot_general(left, right, (((1,), (1,)), ((), ())), preferred_element_...  98.1 us
    dot_general x66, matrix products, dot(): return jnp.dot(left, right, preferred_element_type=f32)  89.6 us
    ppermute x60, waiting for transfers between devices, shift(): return lax.ppermute(value, axis, pairs)  86.5 us
    ppermute x32, waiting for transfers between devices, swap(): return lax.ppermute(value, axis, [(i, i ^ stride) for i in range(size)])  75.1 us
    psum x1, blocking collectives, on_device(): tiny = lax.psum(tiny, 'shard')  75.1 us
    dot_general x38, matrix products, t_dot(): lax.dot_general(left, right, (((0,), (0,)), ((), ())), preferred_element_...  62.5 us
    unnamed x637, local copies, waits for them, and re-layouts  49.7 us
  transfers between devices with their start and end apart: 94, of which 32 were waited for; matrix products, arithmetic and copies ran while one was open for 27% of the time, Pallas kernels for 0%

profile of v1, /device:TPU:0, one launch (start us, length us, event | category | flops | bytes accessed | tf_op | source)
XLA Modules:
  0.0 1065.4 jit_solution(17390633033937988883)
XLA Ops:
  2.8 5.6 collective-permute-start.2
  9.3 4.6 collective-permute-start.38
  35.3 5.8 fusion.438
  41.2 5.8 fusion.430
  53.7 8.5 fusion.441
  63.5 8.5 fusion.433
  85.5 4.8 collective-permute-done.7
  125.2 5.2 collective-permute-start.40
  147.6 6.0 collective-permute-done.33
  155.0 6.1 collective-permute-done.42
  162.4 7.0 collective-permute-done.34
  170.7 5.5 collective-permute-done.43
  205.1 5.2 collective-permute-start.48
  221.5 6.6 collective-permute-done.14
  231.4 10.0 collective-permute-done.44
  251.8 7.7 collective-permute-done.52
  264.4 5.5 collective-permute-done.15
  280.7 7.4 copy.287
  288.1 6.4 reshape.626
  295.7 6.9 fusion.530
  302.6 6.5 fusion.67
  430.2 6.2 multiply_convert_fusion.12
  480.2 10.1 collective-permute-done.85
  502.3 5.2 collective-permute-start.87
  508.0 7.3 copy.322
  515.3 6.4 reshape.630
  540.2 6.5 collective-permute-done.67
  550.4 5.4 fusion.464
  561.0 7.3 copy.326
  568.2 6.6 reshape.631
  574.9 5.3 multiply_reduce_fusion.1
  584.3 5.5 multiply_convert_fusion.7
  591.4 6.3 convolution_bitcast_fusion
  616.1 5.7 multiply_convert_fusion.6
  703.1 4.6 fusion.549
  723.7 8.2 multiply_convert_fusion
  756.3 7.9 subtract_convert_fusion
  778.6 75.1 %psum.15 = f32[33,256]{1,0:T(8,128)S(1)} all-reduce(f32[33,256]{1,0:T(8,128)S(1)} %pad_maximum_fusion.21), channel_id=1, replica_groups=mesh['ctx'=4,'shard'=8] {'shard'}, use_global_device_ids=true, to_apply=%region_10.11 | all-reduce | flops 8448 | bytes 67584 | tf_op jit(solution)/shard_map/psum | solution.py:418
  853.7 5.2 fusion.51
  893.0 5.3 collective-permute-done.70
  899.0 28.0 %collective-permute-done.71 = bf16[4,4,32,2176]{3,2,1,0:T(8,128)(2,1)S(1)} collective-permute-done((bf16[4,4,32,2176]{3,2,1,0:T(8,128)(2,1)}, bf16[4,4,32,2176]{3,2,1,0:T(8,128)(2,1)S(1)}, u32[]{:S(2)}, u32[]{:S(2)}) %collective-permute-start.71) | collective-permute-done | bytes 2228256 | tf_op jit(solution)/shard_map/ppermute | solution.py:52
  937.9 38.3 %psum.14 = f32[1024]{0:T(1024)S(1)} all-reduce(f32[1024]{0:T(1024)S(1)} %get-tuple-element.110), channel_id=1, replica_groups=mesh['ctx'=4,'shard'=8] {'ctx','shard'}, use_global_device_ids=true, to_apply=%region_8.9 | all-reduce | flops 1024 | bytes 8192 | tf_op jit(solution)/shard_map/psum | solution.py:416
  992.5 4.8 collective-permute-done.73
  1005.3 5.1 collective-permute-start.81
  1011.7 4.6 collective-permute-start.74
  1017.8 6.0 collective-permute-done.83
  1028.2 7.5 collective-permute-done.77
  1043.5 13.0 %all-to-all-done = f32[4,32,2176]{2,1,0:T(8,128)} async-done(((f32[4,32,2176]{2,1,0:T(8,128)}), f32[4,32,2176]{2,1,0:T(8,128)}, u32[]{:S(2)}, u32[]{:S(2)}) %all-to-all-start) | async-done | bytes 1114144 | tf_op jit(solution)/shard_map/all_to_all | solution.py:395
  (1179 shorter events, 618.5 us)
Async XLA Ops:
  1.5 74.7 %collective-permute-start.5 = (bf16[34,128]{1,0:T(8,128)(2,1)S(1)}, bf16[34,128]{1,0:T(8,128)(2,1)S(1)}, u32[]{:S(2)}, u32[]{:S(2)}) collective-permute-start(bf16[34,128]{1,0:T(8,128)(2,1)S(1)} %pad_maximum_fusion.22), channel_id=1, source_target_pairs={{2,0},{3,1},{4,2},{5,3},{6,4},{7,5},{10,8},{11,9},{12,10},{13,11},... | collective-permute-start | bytes 26120 | tf_op jit(solution)/shard_map/ppermute | solution.py:47
  2.8 69.9 %collective-permute-start.2 = (bf16[34,128]{1,0:T(8,128)(2,1)S(1)}, bf16[34,128]{1,0:T(8,128)(2,1)S(1)}, u32[]{:S(2)}, u32[]{:S(2)}) collective-permute-start(bf16[34,128]{1,0:T(8,128)(2,1)S(1)} %pad_maximum_fusion.22), channel_id=1, source_target_pairs={{0,2},{1,3},{2,4},{3,5},{4,6},{5,7},{8,10},{9,11},{10,12},{11,13},... | collective-permute-start | bytes 26120 | tf_op jit(solution)/shard_map/ppermute | solution.py:47
  9.3 104.4 %collective-permute-start.38 = (bf16[32,2048]{1,0:T(8,128)(2,1)S(1)}, bf16[32,2048]{1,0:T(8,128)(2,1)}, u32[]{:S(2)}, u32[]{:S(2)}) collective-permute-start(bf16[32,2048]{1,0:T(8,128)(2,1)S(1)} %fusion.387), channel_id=1, source_target_pairs={{0,2},{1,3},{2,4},{3,5},{4,6},{5,7},{8,10},{9,11},{10,12},{11,13},... | collective-permute-start | bytes 393224 | tf_op jit(solution)/shard_map/ppermute | solution.py:47
  13.8 131.6 %collective-permute-start.41 = (bf16[32,2048]{1,0:T(8,128)(2,1)S(1)}, bf16[32,2048]{1,0:T(8,128)(2,1)}, u32[]{:S(2)}, u32[]{:S(2)}) collective-permute-start(bf16[32,2048]{1,0:T(8,128)(2,1)S(1)} %fusion.387), channel_id=1, source_target_pairs={{2,0},{3,1},{4,2},{5,3},{6,4},{7,5},{10,8},{11,9},{12,10},{13,11},... | collective-permute-start | bytes 393224 | tf_op jit(solution)/shard_map/ppermute | solution.py:47
  28.8 76.3 %collective-permute-start.29 = (bf16[32,2048]{1,0:T(8,128)(2,1)S(1)}, bf16[32,2048]{1,0:T(8,128)(2,1)S(1)}, u32[]{:S(2)}, u32[]{:S(2)}) collective-permute-start(bf16[32,2048]{1,0:T(8,128)(2,1)S(1)} %fusion.388), channel_id=1, source_target_pairs={{0,2},{1,3},{2,4},{3,5},{4,6},{5,7},{8,10},{9,11},{10,12},{11,13},... | collective-permute-start | bytes 393224 | tf_op jit(solution)/shard_map/ppermute | solution.py:47
  82.8 61.0 %collective-permute-start.32 = (bf16[32,2048]{1,0:T(8,128)(2,1)S(1)}, bf16[32,2048]{1,0:T(8,128)(2,1)S(1)}, u32[]{:S(2)}, u32[]{:S(2)}) collective-permute-start(bf16[32,2048]{1,0:T(8,128)(2,1)S(1)} %fusion.388), channel_id=1, source_target_pairs={{2,0},{3,1},{4,2},{5,3},{6,4},{7,5},{10,8},{11,9},{12,10},{13,11},... | collective-permute-start | bytes 393224 | tf_op jit(solution)/shard_map/ppermute | solution.py:47
  122.6 65.8 %collective-permute-start.57 = (bf16[88,1024]{1,0:T(8,128)(2,1)S(1)}, bf16[88,1024]{1,0:T(8,128)(2,1)S(1)}, u32[]{:S(2)}, u32[]{:S(2)}) collective-permute-start(bf16[88,1024]{1,0:T(8,128)(2,1)S(1)} %copy-done.190), channel_id=1, source_target_pairs={{2,0},{3,1},{4,2},{5,3},{6,4},{7,5},{10,8},{11,9},{12,10},{13,11},... | collective-permute-start | bytes 540680 | tf_op jit(solution)/shard_map/ppermute | solution.py:47
  132.5 45.2 %collective-permute-start.54 = (bf16[88,1024]{1,0:T(8,128)(2,1)S(1)}, bf16[88,1024]{1,0:T(8,128)(2,1)S(1)}, u32[]{:S(2)}, u32[]{:S(2)}) collective-permute-start(bf16[88,1024]{1,0:T(8,128)(2,1)S(1)} %copy-done.190), channel_id=1, source_target_pairs={{0,2},{1,3},{2,4},{3,5},{4,6},{5,7},{8,10},{9,11},{10,12},{11,13},... | collective-permute-start | bytes 540680 | tf_op jit(solution)/shard_map/ppermute | solution.py:47
  143.3 39.0 %collective-permute-start.63 = (bf16[256,1024]{1,0:T(8,128)(2,1)S(1)}, bf16[256,1024]{1,0:T(8,128)(2,1)S(1)}, u32[]{:S(2)}, u32[]{:S(2)}) collective-permute-start(bf16[256,1024]{1,0:T(8,128)(2,1)S(1)} %bitcast.943), channel_id=1, source_target_pairs={{0,16},{8,24},{16,0},{24,8},{1,17},{9,25},{17,1},{25,9},{2,18},{10... | collective-permute-start | bytes 1572872 | tf_op jit(solution)/shard_map/ppermute | solution.py:52
  143.8 39.8 %collective-permute-start = (bf16[256,1024]{1,0:T(8,128)(2,1)S(1)}, bf16[256,1024]{1,0:T(8,128)(2,1)S(1)}, u32[]{:S(2)}, u32[]{:S(2)}) collective-permute-start(bf16[256,1024]{1,0:T(8,128)(2,1)S(1)} %bitcast.944), channel_id=1, source_target_pairs={{0,16},{8,24},{16,0},{24,8},{1,17},{9,25},{17,1},{25,9},{2,18},{10... | collective-permute-start | bytes 1572872 | tf_op jit(solution)/shard_map/ppermute | solution.py:52
  176.2 26.3 %collective-permute-start.50 = (bf16[128,1408]{0,1:T(8,128)(2,1)S(1)}, bf16[128,1408]{0,1:T(8,128)(2,1)S(1)}, u32[]{:S(2)}, u32[]{:S(2)}) collective-permute-start(bf16[128,1408]{0,1:T(8,128)(2,1)S(1)} %pad_maximum_fusion.19), channel_id=1, source_target_pairs={{2,0},{3,1},{4,2},{5,3},{6,4},{7,5},{10,8},{11,9},{12,10},{13,11},... | collective-permute-start | bytes 1081352 | tf_op jit(solution)/shard_map/ppermute | solution.py:47
  177.7 26.1 %collective-permute-start.47 = (bf16[128,1408]{0,1:T(8,128)(2,1)S(1)}, bf16[128,1408]{0,1:T(8,128)(2,1)S(1)}, u32[]{:S(2)}, u32[]{:S(2)}) collective-permute-start(bf16[128,1408]{0,1:T(8,128)(2,1)S(1)} %pad_maximum_fusion.19), channel_id=1, source_target_pairs={{0,2},{1,3},{2,4},{3,5},{4,6},{5,7},{8,10},{9,11},{10,12},{11,13},... | collective-permute-start | bytes 1081352 | tf_op jit(solution)/shard_map/ppermute | solution.py:47
  196.6 20.3 %collective-permute-start.13 = (bf16[128,768]{1,0:T(8,128)(2,1)S(1)}, bf16[128,768]{1,0:T(8,128)(2,1)S(1)}, u32[]{:S(2)}, u32[]{:S(2)}) collective-permute-start(bf16[128,768]{1,0:T(8,128)(2,1)S(1)} %collective-permute-done.12), channel_id=1, source_target_pairs={{2,0},{3,1},{4,2},{5,3},{6,4},{7,5},{10,8},{11,9},{12,10},{13,11},... | collective-permute-start | bytes 589832 | tf_op jit(solution)/shard_map/ppermute | solution.py:47
  203.8 42.4 %collective-permute-start.51 = (bf16[128,1408]{0,1:T(8,128)(2,1)S(1)}, bf16[128,1408]{0,1:T(8,128)(2,1)S(1)}, u32[]{:S(2)}, u32[]{:S(2)}) collective-permute-start(bf16[128,1408]{0,1:T(8,128)(2,1)S(1)} %collective-permute-done.50), channel_id=1, source_target_pairs={{2,0},{3,1},{4,2},{5,3},{6,4},{7,5},{10,8},{11,9},{12,10},{13,11},... | collective-permute-start | bytes 1081352 | tf_op jit(solution)/shard_map/ppermute | solution.py:47
  205.1 24.7 %collective-permute-start.48 = (bf16[128,1408]{0,1:T(8,128)(2,1)S(1)}, bf16[128,1408]{0,1:T(8,128)(2,1)S(1)}, u32[]{:S(2)}, u32[]{:S(2)}) collective-permute-start(bf16[128,1408]{0,1:T(8,128)(2,1)S(1)} %collective-permute-done.47), channel_id=1, source_target_pairs={{0,2},{1,3},{2,4},{3,5},{4,6},{5,7},{8,10},{9,11},{10,12},{11,13},... | collective-permute-start | bytes 1081352 | tf_op jit(solution)/shard_map/ppermute | solution.py:47
  211.4 17.3 %collective-permute-start.26 = (bf16[4,32,2048]{2,1,0:T(8,128)(2,1)S(1)}, bf16[4,32,2048]{2,1,0:T(8,128)(2,1)S(1)}, u32[]{:S(2)}, u32[]{:S(2)}) collective-permute-start(bf16[4,32,2048]{2,1,0:T(8,128)(2,1)S(1)} %constant_dynamic-slice_fusion.13), channel_id=1, source_target_pairs={{0,1},{1,0},{2,3},{3,2},{4,5},{5,4},{6,7},{7,6},{8,9},{9,8},{10,11... | collective-permute-start | bytes 1572872 | tf_op jit(solution)/shard_map/ppermute | solution.py:52
  228.7 41.7 %collective-permute-start.1 = (bf16[2,256,1024]{2,1,0:T(8,128)(2,1)S(1)}, bf16[2,256,1024]{2,1,0:T(8,128)(2,1)S(1)}, u32[]{:S(2)}, u32[]{:S(2)}) collective-permute-start(bf16[2,256,1024]{2,1,0:T(8,128)(2,1)S(1)} %pad_maximum_fusion.6), channel_id=1, source_target_pairs={{0,8},{8,0},{16,24},{24,16},{1,9},{9,1},{17,25},{25,17},{2,10},{10... | collective-permute-start | bytes 3145736 | tf_op jit(solution)/shard_map/ppermute | solution.py:52
  229.6 44.5 %collective-permute-start.64 = (bf16[2,256,1024]{2,1,0:T(8,128)(2,1)S(1)}, bf16[2,256,1024]{2,1,0:T(8,128)(2,1)S(1)}, u32[]{:S(2)}, u32[]{:S(2)}) collective-permute-start(bf16[2,256,1024]{2,1,0:T(8,128)(2,1)S(1)} %pad_maximum_fusion.11), channel_id=1, source_target_pairs={{0,8},{8,0},{16,24},{24,16},{1,9},{9,1},{17,25},{25,17},{2,10},{10... | collective-permute-start | bytes 3145736 | tf_op jit(solution)/shard_map/ppermute | solution.py:52
  229.8 31.6 %collective-permute-start.60 = (bf16[4,88,1024]{2,1,0:T(8,128)(2,1)S(1)}, bf16[4,88,1024]{2,1,0:T(8,128)(2,1)S(1)}, u32[]{:S(2)}, u32[]{:S(2)}) collective-permute-start(bf16[4,88,1024]{2,1,0:T(8,128)(2,1)S(1)} %constant_dynamic-slice_fusion.5), channel_id=1, source_target_pairs={{0,1},{1,0},{2,3},{3,2},{4,5},{5,4},{6,7},{7,6},{8,9},{9,8},{10,11... | collective-permute-start | bytes 2162696 | tf_op jit(solution)/shard_map/ppermute | solution.py:52
  246.3 23.7 %collective-permute-start.15 = (bf16[4,128,768]{2,1,0:T(8,128)(2,1)S(1)}, bf16[4,128,768]{2,1,0:T(8,128)(2,1)S(1)}, u32[]{:S(2)}, u32[]{:S(2)}) collective-permute-start(bf16[4,128,768]{2,1,0:T(8,128)(2,1)S(1)} %constant_dynamic-slice_fusion.15), channel_id=1, source_target_pairs={{0,1},{1,0},{2,3},{3,2},{4,5},{5,4},{6,7},{7,6},{8,9},{9,8},{10,11... | collective-permute-start | bytes 2359304 | tf_op jit(solution)/shard_map/ppermute | solution.py:52
  259.5 56.5 %collective-permute-start.45 = (bf16[256,2048]{1,0:T(8,128)(2,1)}, bf16[256,2048]{1,0:T(8,128)(2,1)}, u32[]{:S(2)}, u32[]{:S(2)}) collective-permute-start(bf16[256,2048]{1,0:T(8,128)(2,1)} %bitcast.135), channel_id=1, source_target_pairs={{0,16},{8,24},{16,0},{24,8},{1,17},{9,25},{17,1},{25,9},{2,18},{10... | collective-permute-start | bytes 3145736 | tf_op jit(solution)/shard_map/ppermute | solution.py:52
  261.4 58.3 %collective-permute-start.36 = (bf16[256,2048]{1,0:T(8,128)(2,1)S(1)}, bf16[256,2048]{1,0:T(8,128)(2,1)}, u32[]{:S(2)}, u32[]{:S(2)}) collective-permute-start(bf16[256,2048]{1,0:T(8,128)(2,1)S(1)} %bitcast.906), channel_id=1, source_target_pairs={{0,16},{8,24},{16,0},{24,8},{1,17},{9,25},{17,1},{25,9},{2,18},{10... | collective-permute-start | bytes 3145736 | tf_op jit(solution)/shard_map/ppermute | solution.py:52
  270.0 55.3 %collective-permute-start.27 = (bf16[256,2048]{1,0:T(8,128)(2,1)S(1)}, bf16[256,2048]{1,0:T(8,128)(2,1)}, u32[]{:S(2)}, u32[]{:S(2)}) collective-permute-start(bf16[256,2048]{1,0:T(8,128)(2,1)S(1)} %bitcast.905), channel_id=1, source_target_pairs={{0,16},{8,24},{16,0},{24,8},{1,17},{9,25},{17,1},{25,9},{2,18},{10... | collective-permute-start | bytes 3145736 | tf_op jit(solution)/shard_map/ppermute | solution.py:52
  270.4 64.3 %collective-permute-start.53 = (bf16[4,128,1408]{1,2,0:T(8,128)(2,1)}, bf16[4,128,1408]{1,2,0:T(8,128)(2,1)}, u32[]{:S(2)}, u32[]{:S(2)}) collective-permute-start(bf16[4,128,1408]{1,2,0:T(8,128)(2,1)} %constant_dynamic-slice_fusion.7), channel_id=1, source_target_pairs={{0,1},{1,0},{2,3},{3,2},{4,5},{5,4},{6,7},{7,6},{8,9},{9,8},{10,11... | collective-permute-start | bytes 4325384 | tf_op jit(solution)/shard_map/ppermute | solution.py:52
  310.4 20.4 %collective-permute-start.16 = (bf16[1,1024,256]{2,1,0:T(8,128)(2,1)S(1)}, bf16[1,1024,256]{2,1,0:T(8,128)(2,1)S(1)}, u32[]{:S(2)}, u32[]{:S(2)}) collective-permute-start(bf16[1,1024,256]{2,1,0:T(8,128)(2,1)S(1)} %copy.295), channel_id=1, source_target_pairs={{0,16},{8,24},{16,0},{24,8},{1,17},{9,25},{17,1},{25,9},{2,18},{10... | collective-permute-start | bytes 1572872 | tf_op jit(solution)/shard_map/ppermute | solution.py:52
  319.7 22.9 %collective-permute-start.46 = (bf16[2,256,2048]{2,1,0:T(8,128)(2,1)}, bf16[2,256,2048]{2,1,0:T(8,128)(2,1)}, u32[]{:S(2)}, u32[]{:S(2)}) collective-permute-start(bf16[2,256,2048]{2,1,0:T(8,128)(2,1)} %pad_maximum_fusion.5), channel_id=1, source_target_pairs={{0,8},{8,0},{16,24},{24,16},{1,9},{9,1},{17,25},{25,17},{2,10},{10... | collective-permute-start | bytes 6291464 | tf_op jit(solution)/shard_map/ppermute | solution.py:52
  323.1 24.7 %collective-permute-start.37 = (bf16[2,256,2048]{2,1,0:T(8,128)(2,1)}, bf16[2,256,2048]{2,1,0:T(8,128)(2,1)}, u32[]{:S(2)}, u32[]{:S(2)}) collective-permute-start(bf16[2,256,2048]{2,1,0:T(8,128)(2,1)} %pad_maximum_fusion.4), channel_id=1, source_target_pairs={{0,8},{8,0},{16,24},{24,16},{1,9},{9,1},{17,25},{25,17},{2,10},{10... | collective-permute-start | bytes 6291464 | tf_op jit(solution)/shard_map/ppermute | solution.py:52
  334.3 80.2 %collective-permute-start.28 = (bf16[2,256,2048]{2,1,0:T(8,128)(2,1)}, bf16[2,256,2048]{2,1,0:T(8,128)(2,1)}, u32[]{:S(2)}, u32[]{:S(2)}) collective-permute-start(bf16[2,256,2048]{2,1,0:T(8,128)(2,1)} %pad_maximum_fusion.3), channel_id=1, source_target_pairs={{0,8},{8,0},{16,24},{24,16},{1,9},{9,1},{17,25},{25,17},{2,10},{10... | collective-permute-start | bytes 6291464 | tf_op jit(solution)/shard_map/ppermute | solution.py:52
  463.1 34.0 %collective-permute-start.65 = (bf16[2,256,1024]{2,1,0:T(8,128)(2,1)}, bf16[2,256,1024]{2,1,0:T(8,128)(2,1)}, u32[]{:S(2)}, u32[]{:S(2)}) collective-permute-start(bf16[2,256,1024]{2,1,0:T(8,128)(2,1)} %fusion.190), channel_id=1, source_target_pairs={{0,8},{8,0},{16,24},{24,16},{1,9},{9,1},{17,25},{25,17},{2,10},{10... | collective-permute-start | bytes 3145736 | tf_op jit(solution)/shard_map/ppermute | solution.py:52
  472.0 18.4 %collective-permute-start.85 = (bf16[4,88,1024]{2,1,0:T(8,128)(2,1)}, bf16[4,88,1024]{2,1,0:T(8,128)(2,1)}, u32[]{:S(2)}, u32[]{:S(2)}) collective-permute-start(bf16[4,88,1024]{2,1,0:T(8,128)(2,1)} %fusion.217), channel_id=1, source_target_pairs={{0,1},{1,0},{2,3},{3,2},{4,5},{5,4},{6,7},{7,6},{8,9},{9,8},{10,11... | collective-permute-start | bytes 2162696 | tf_op jit(solution)/shard_map/ppermute | solution.py:52
  480.2 53.1 %collective-permute-start.61 = (bf16[2,256,1024]{1,2,0:T(8,128)(2,1)}, bf16[2,256,1024]{1,2,0:T(8,128)(2,1)S(1)}, u32[]{:S(2)}, u32[]{:S(2)}) collective-permute-start(bf16[2,256,1024]{1,2,0:T(8,128)(2,1)} %bitcast.941), channel_id=1, source_target_pairs={{0,8},{8,0},{16,24},{24,16},{1,9},{9,1},{17,25},{25,17},{2,10},{10... | collective-permute-start | bytes 3145736 | tf_op jit(solution)/shard_map/ppermute | solution.py:52
  495.8 32.1 %collective-permute-start.89 = (bf16[88,1024]{1,0:T(8,128)(2,1)S(1)}, bf16[88,1024]{1,0:T(8,128)(2,1)S(1)}, u32[]{:S(2)}, u32[]{:S(2)}) collective-permute-start(bf16[88,1024]{1,0:T(8,128)(2,1)S(1)} %get-tuple-element.206), channel_id=1, source_target_pairs={{2,0},{3,1},{4,2},{5,3},{6,4},{7,5},{10,8},{11,9},{12,10},{13,11},... | collective-permute-start | bytes 540680 | tf_op jit(solution)/shard_map/ppermute | solution.py:47
  501.1 29.3 %collective-permute-start.66 = (bf16[256,1024]{1,0:T(8,128)(2,1)}, bf16[256,1024]{1,0:T(8,128)(2,1)S(1)}, u32[]{:S(2)}, u32[]{:S(2)}) collective-permute-start(bf16[256,1024]{1,0:T(8,128)(2,1)} %fusion.263), channel_id=1, source_target_pairs={{0,16},{8,24},{16,0},{24,8},{1,17},{9,25},{17,1},{25,9},{2,18},{10... | collective-permute-start | bytes 1572872 | tf_op jit(solution)/shard_map/ppermute | solution.py:52
  502.3 25.6 %collective-permute-start.87 = (bf16[88,1024]{1,0:T(8,128)(2,1)}, bf16[88,1024]{1,0:T(8,128)(2,1)}, u32[]{:S(2)}, u32[]{:S(2)}) collective-permute-start(bf16[88,1024]{1,0:T(8,128)(2,1)} %fusion.357), channel_id=1, source_target_pairs={{0,2},{1,3},{2,4},{3,5},{4,6},{5,7},{8,10},{9,11},{10,12},{11,13},... | collective-permute-start | bytes 540680 | tf_op jit(solution)/shard_map/ppermute | solution.py:47
  533.7 22.2 %collective-permute-start.62 = (bf16[256,1024]{0,1:T(8,128)(2,1)S(1)}, bf16[256,1024]{0,1:T(8,128)(2,1)S(1)}, u32[]{:S(2)}, u32[]{:S(2)}) collective-permute-start(bf16[256,1024]{0,1:T(8,128)(2,1)S(1)} %fusion.262), channel_id=1, source_target_pairs={{0,16},{8,24},{16,0},{24,8},{1,17},{9,25},{17,1},{25,9},{2,18},{10... | collective-permute-start | bytes 1572872 | tf_op jit(solution)/shard_map/ppermute | solution.py:52
  774.1 111.4 %collective-permute-start.78 = (bf16[4,32,6144]{2,1,0:T(8,128)(2,1)}, bf16[4,32,6144]{2,1,0:T(8,128)(2,1)}, u32[]{:S(2)}, u32[]{:S(2)}) collective-permute-start(bf16[4,32,6144]{2,1,0:T(8,128)(2,1)} %fusion.44), channel_id=1, source_target_pairs={{0,1},{1,0},{2,3},{3,2},{4,5},{5,4},{6,7},{7,6},{8,9},{9,8},{10,11... | collective-permute-start | bytes 4718600 | tf_op jit(solution)/shard_map/ppermute | solution.py:52
  875.9 51.1 %collective-permute-start.71 = (bf16[4,4,32,2176]{3,2,1,0:T(8,128)(2,1)}, bf16[4,4,32,2176]{3,2,1,0:T(8,128)(2,1)S(1)}, u32[]{:S(2)}, u32[]{:S(2)}) collective-permute-start(bf16[4,4,32,2176]{3,2,1,0:T(8,128)(2,1)} %fusion.18), channel_id=1, source_target_pairs={{0,1},{1,0},{2,3},{3,2},{4,5},{5,4},{6,7},{7,6},{8,9},{9,8},{10,11... | collective-permute-start | bytes 6684680 | tf_op jit(solution)/shard_map/ppermute | solution.py:52
  889.7 94.5 %collective-permute-start.79 = (bf16[32,6144]{1,0:T(8,128)(2,1)}, bf16[32,6144]{1,0:T(8,128)(2,1)}, u32[]{:S(2)}, u32[]{:S(2)}) collective-permute-start(bf16[32,6144]{1,0:T(8,128)(2,1)} %get-tuple-element.180), channel_id=1, source_target_pairs={{0,2},{1,3},{2,4},{3,5},{4,6},{5,7},{8,10},{9,11},{10,12},{11,13},... | collective-permute-start | bytes 1179656 | tf_op jit(solution)/shard_map/ppermute | solution.py:47
  891.8 108.7 %collective-permute-start.82 = (bf16[32,6144]{1,0:T(8,128)(2,1)}, bf16[32,6144]{1,0:T(8,128)(2,1)}, u32[]{:S(2)}, u32[]{:S(2)}) collective-permute-start(bf16[32,6144]{1,0:T(8,128)(2,1)} %get-tuple-element.181), channel_id=1, source_target_pairs={{2,0},{3,1},{4,2},{5,3},{6,4},{7,5},{10,8},{11,9},{12,10},{13,11},... | collective-permute-start | bytes 1179656 | tf_op jit(solution)/shard_map/ppermute | solution.py:47
  930.8 47.4 %collective-permute-start.72 = (bf16[4,32,2176]{2,1,0:T(8,128)(2,1)}, bf16[4,32,2176]{2,1,0:T(8,128)(2,1)}, u32[]{:S(2)}, u32[]{:S(2)}) collective-permute-start(bf16[4,32,2176]{2,1,0:T(8,128)(2,1)} %get-tuple-element.170), channel_id=1, source_target_pairs={{0,2},{1,3},{2,4},{3,5},{4,6},{5,7},{8,10},{9,11},{10,12},{11,13},... | collective-permute-start | bytes 1671176 | tf_op jit(solution)/shard_map/ppermute | solution.py:47
  979.7 17.6 %collective-permute-start.73 = (bf16[4,32,2176]{2,1,0:T(8,128)(2,1)S(1)}, bf16[4,32,2176]{2,1,0:T(8,128)(2,1)S(1)}, u32[]{:S(2)}, u32[]{:S(2)}) collective-permute-start(bf16[4,32,2176]{2,1,0:T(8,128)(2,1)S(1)} %fusion.187), channel_id=1, source_target_pairs={{0,2},{1,3},{2,4},{3,5},{4,6},{5,7},{8,10},{9,11},{10,12},{11,13},... | collective-permute-start | bytes 1671176 | tf_op jit(solution)/shard_map/ppermute | solution.py:47
  985.5 17.9 %collective-permute-start.80 = (bf16[32,6144]{1,0:T(8,128)(2,1)S(1)}, bf16[32,6144]{1,0:T(8,128)(2,1)S(1)}, u32[]{:S(2)}, u32[]{:S(2)}) collective-permute-start(bf16[32,6144]{1,0:T(8,128)(2,1)S(1)} %fusion.214), channel_id=1, source_target_pairs={{0,2},{1,3},{2,4},{3,5},{4,6},{5,7},{8,10},{9,11},{10,12},{11,13},... | collective-permute-start | bytes 1179656 | tf_op jit(solution)/shard_map/ppermute | solution.py:47
  999.1 17.2 %collective-permute-start.76 = (bf16[4,32,2176]{2,1,0:T(8,128)(2,1)S(1)}, bf16[4,32,2176]{2,1,0:T(8,128)(2,1)S(1)}, u32[]{:S(2)}, u32[]{:S(2)}) collective-permute-start(bf16[4,32,2176]{2,1,0:T(8,128)(2,1)S(1)} %get-tuple-element.169), channel_id=1, source_target_pairs={{2,0},{3,1},{4,2},{5,3},{6,4},{7,5},{10,8},{11,9},{12,10},{13,11},... | collective-permute-start | bytes 1671176 | tf_op jit(solution)/shard_map/ppermute | solution.py:47
  1005.3 35.9 %collective-permute-start.81 = (bf16[32,6144]{1,0:T(8,128)(2,1)}, bf16[32,6144]{1,0:T(8,128)(2,1)}, u32[]{:S(2)}, u32[]{:S(2)}) collective-permute-start(bf16[32,6144]{1,0:T(8,128)(2,1)} %get-tuple-element.178), channel_id=1, source_target_pairs={{0,2},{1,3},{2,4},{3,5},{4,6},{5,7},{8,10},{9,11},{10,12},{11,13},... | collective-permute-start | bytes 1179656 | tf_op jit(solution)/shard_map/ppermute | solution.py:47
  1011.7 16.5 %collective-permute-start.74 = (bf16[4,32,2176]{2,1,0:T(8,128)(2,1)S(1)}, bf16[4,32,2176]{2,1,0:T(8,128)(2,1)S(1)}, u32[]{:S(2)}, u32[]{:S(2)}) collective-permute-start(bf16[4,32,2176]{2,1,0:T(8,128)(2,1)S(1)} %get-tuple-element.168), channel_id=1, source_target_pairs={{0,2},{1,3},{2,4},{3,5},{4,6},{5,7},{8,10},{9,11},{10,12},{11,13},... | collective-permute-start | bytes 1671176 | tf_op jit(solution)/shard_map/ppermute | solution.py:47
  1016.5 19.2 %collective-permute-start.77 = (bf16[4,32,2176]{2,1,0:T(8,128)(2,1)S(1)}, bf16[4,32,2176]{2,1,0:T(8,128)(2,1)S(1)}, u32[]{:S(2)}, u32[]{:S(2)}) collective-permute-start(bf16[4,32,2176]{2,1,0:T(8,128)(2,1)S(1)} %fusion.186), channel_id=1, source_target_pairs={{2,0},{3,1},{4,2},{5,3},{6,4},{7,5},{10,8},{11,9},{12,10},{13,11},... | collective-permute-start | bytes 1671176 | tf_op jit(solution)/shard_map/ppermute | solution.py:47
  1024.6 16.8 %collective-permute-start.84 = (bf16[32,6144]{1,0:T(8,128)(2,1)}, bf16[32,6144]{1,0:T(8,128)(2,1)}, u32[]{:S(2)}, u32[]{:S(2)}) collective-permute-start(bf16[32,6144]{1,0:T(8,128)(2,1)} %fusion.213), channel_id=1, source_target_pairs={{2,0},{3,1},{4,2},{5,3},{6,4},{7,5},{10,8},{11,9},{12,10},{13,11},... | collective-permute-start | bytes 1179656 | tf_op jit(solution)/shard_map/ppermute | solution.py:47
  1037.0 19.5 %all-to-all-start = ((f32[4,32,2176]{2,1,0:T(8,128)}), f32[4,32,2176]{2,1,0:T(8,128)}, u32[]{:S(2)}, u32[]{:S(2)}) async-start(f32[4,32,2176]{2,1,0:T(8,128)} %fusion.189), calls=%async_computation | async-start | bytes 2228224 | tf_op jit(solution)/shard_map/all_to_all | solution.py:395
  (324 other events, 4318.7 us)
